TPU v7x, 512 devices: a whole 4x4x16 slice. The times are simulated.
512 devices in a mesh: gx: 32 (over z_lo, y, core), gy: 16 (over z_hi, x).
Axes of the slice: x: 4, y: 4, z: 16 (z_hi: 4, z_lo: 4; z = z_hi * 4 + z_lo), core: 2. Of those that a mesh axis runs over, the one named last changes fastest.
Arguments:
- current: bfloat16 [4, 256, 256, 128], P(None, 'gx', 'gy'), may hold values from -6 to 6
- previous: bfloat16 [4, 256, 256, 128], P(None, 'gx', 'gy'), may hold values from -6 to 6
- offsets: int32 [4, 2], replicated, may hold values from -6 to 6, as said below
- center_rows: int32 [4, 64], replicated, may hold values from 0 to 255
- center_cols: int32 [4, 64], replicated, may hold values from 0 to 255
- classes: int32 [4, 64], replicated, may hold values from 0 to 9
- w_merge1: bfloat16 [3, 3, 256, 128], replicated, may hold values from -0.125 to 0.125
- w_merge2: bfloat16 [3, 3, 128, 128], replicated, may hold values from -0.1875 to 0.1875
- w_head: bfloat16 [128, 10], replicated, may hold values from -0.5 to 0.5
Outputs:
- loss: float32 [], replicated
- grad_merge1: float32 [3, 3, 256, 128], replicated
- grad_merge2: float32 [3, 3, 128, 128], replicated
- grad_head: float32 [128, 10], replicated
- grad_current: bfloat16 [4, 256, 256, 128], P(None, 'gx', 'gy')
- grad_previous: bfloat16 [4, 256, 256, 128], P(None, 'gx', 'gy')
Inputs may be any that keep to these rules, and one draw needn't show every extreme that they name: `offsets`: no offset is zero; along each of the two axes half of the scenes have a positive offset and half a negative one; in every draw some offset has magnitude exactly 6.
All inputs are finite; a program needn't handle non-finite values.
Results may differ from a plain program's by a relative error of at most 0.0085.
Values may be sent and summed in bfloat16 or wider, within the bound.
A program may use at most 64 MiB of HBM per device.

v0:
```python
import jax
import jax.numpy as jnp
from jax import lax
from jax.sharding import PartitionSpec as P


def extended(block, sides, width):
    for axis, dim in sides:
        count = lax.axis_size(axis)
        forward = [(i, i + 1) for i in range(count - 1)]
        backward = [(target, source) for source, target in forward]
        low = lax.ppermute(
            lax.slice_in_dim(block, block.shape[dim] - width, None, axis=dim), axis, forward
        )
        high = lax.ppermute(lax.slice_in_dim(block, 0, width, axis=dim), axis, backward)
        block = jnp.concatenate([low, block, high], axis=dim)
    return block


def silu_grad(value):
    sig = jax.nn.sigmoid(value)
    return sig * (1.0 + value * (1.0 - sig))


def convolve(padded, weight, rows, cols):
    total = jnp.zeros((padded.shape[0] * rows * cols, weight.shape[3]), jnp.float32)
    for i in range(3):
        for j in range(3):
            window = padded[:, i : i + rows, j : j + cols].reshape(-1, padded.shape[3])
            total = total + jnp.dot(window, weight[i, j], preferred_element_type=jnp.float32)
    return total


def back_convolve(padded, weight, rows, cols):
    total = jnp.zeros((padded.shape[0] * rows * cols, weight.shape[2]), jnp.float32)
    for i in range(3):
        for j in range(3):
            window = padded[:, 2 - i : 2 - i + rows, 2 - j : 2 - j + cols].reshape(
                -1, padded.shape[3]
            )
            total = total + jnp.dot(window, weight[i, j].T, preferred_element_type=jnp.float32)
    return total


def weight_grad(padded, upstream, rows, cols):
    taps = []
    for i in range(3):
        for j in range(3):
            window = padded[:, i : i + rows, j : j + cols].reshape(-1, padded.shape[3])
            taps.append(
                lax.dot_general(
                    window, upstream, (((0,), (0,)), ((), ())), preferred_element_type=jnp.float32
                )
            )
    return jnp.stack(taps).reshape(3, 3, padded.shape[3], upstream.shape[1])


def focal(logits, target, positive, count):
    prob = jax.nn.sigmoid(logits)
    log_p = jax.nn.log_sigmoid(logits)
    log_q = jax.nn.log_sigmoid(-logits)
    miss = 1.0 - target
    miss = miss * miss
    pos_term = -(1.0 - prob) * (1.0 - prob) * log_p
    neg_term = -(miss * miss) * prob * prob * log_q
    return jnp.sum(jnp.where(positive, pos_term, neg_term)) / count


def select_cells(wide, offsets, sign, span, rows, cols, chans):

    def one_scene(field, offset):
        zero = jnp.zeros((), jnp.int32)
        start_r = span + sign * offset[0]
        start_c = span + sign * offset[1]
        return lax.dynamic_slice(field, (start_r, start_c, zero), (rows, cols, chans))

    return jax.vmap(one_scene)(wide, offsets)


def per_device(
    current, previous, offsets, center_rows, center_cols, classes, w_merge1, w_merge2, w_head
):
    scenes, rows, cols, chans = current.shape
    n_cls = w_head.shape[1]
    count = center_rows.shape[0] * center_rows.shape[1]
    span = min(rows, cols) * 3 // 4
    row_start = lax.axis_index("gx") * rows
    col_start = lax.axis_index("gy") * cols
    wide = extended(previous, (("gx", 1), ("gy", 2)), span)
    aligned = select_cells(wide, offsets, -1, span, rows, cols, chans)
    stacked = jnp.concatenate([current, aligned], axis=3)
    stack_ext = extended(stacked, (("gx", 1), ("gy", 2)), 1)
    pre1 = convolve(stack_ext, w_merge1, rows, cols)
    hidden1 = jax.nn.silu(pre1).astype(jnp.bfloat16).reshape(scenes, rows, cols, chans)
    hid_ext = extended(hidden1, (("gx", 1), ("gy", 2)), 1)
    pre2 = convolve(hid_ext, w_merge2, rows, cols)
    hidden2 = jax.nn.silu(pre2).astype(jnp.bfloat16)
    logits = (jnp.dot(hidden2, w_head, preferred_element_type=jnp.float32) - 2.19).reshape(
        scenes, rows, cols, n_cls
    )
    grid_row_ids = row_start + jnp.arange(rows, dtype=jnp.int32)
    grid_col_ids = col_start + jnp.arange(cols, dtype=jnp.int32)
    onehot = (classes[:, :, None] == jnp.arange(n_cls, dtype=jnp.int32)[None, None, :]).astype(
        jnp.float32
    )
    dr = (grid_row_ids[None, :, None] - center_rows[:, None, :]).astype(jnp.float32)
    dc = (grid_col_ids[None, :, None] - center_cols[:, None, :]).astype(jnp.float32)
    bump = jnp.exp(-(dr * dr)[:, :, None, :] / 8.0 - (dc * dc)[:, None, :, :] / 8.0)
    target = jnp.max(bump[..., None] * onehot[:, None, None, :, :], axis=3)
    hit = (
        (grid_row_ids[None, :, None] == center_rows[:, None, :])[:, :, None, :]
        & (grid_col_ids[None, :, None] == center_cols[:, None, :])[:, None, :, :]
    ).astype(jnp.float32)
    positive = jnp.einsum("srco,sok->srck", hit, onehot) > 0.5
    loss_part, back = jax.vjp(lambda z: focal(z, target, positive, count), logits)
    d_logits = back(jnp.ones((), jnp.float32))[0].astype(jnp.bfloat16).reshape(-1, n_cls)
    head_part = lax.dot_general(
        hidden2, d_logits, (((0,), (0,)), ((), ())), preferred_element_type=jnp.float32
    )
    d_hid2 = jnp.dot(d_logits, w_head.T, preferred_element_type=jnp.float32)
    d_pre2 = (d_hid2 * silu_grad(pre2)).astype(jnp.bfloat16)
    merge2_part = weight_grad(hid_ext, d_pre2, rows, cols)
    dpad2 = extended(d_pre2.reshape(scenes, rows, cols, chans), (("gx", 1), ("gy", 2)), 1)
    d_hid1 = back_convolve(dpad2, w_merge2, rows, cols)
    d_pre1 = (d_hid1 * silu_grad(pre1)).astype(jnp.bfloat16)
    merge1_part = weight_grad(stack_ext, d_pre1, rows, cols)
    dpad1 = extended(d_pre1.reshape(scenes, rows, cols, chans), (("gx", 1), ("gy", 2)), 1)
    d_stack = back_convolve(dpad1, w_merge1, rows, cols).reshape(scenes, rows, cols, 2 * chans)
    grad_current = d_stack[..., :chans].astype(jnp.bfloat16)
    d_aligned = d_stack[..., chans:].astype(jnp.bfloat16)
    back_wide = extended(d_aligned, (("gx", 1), ("gy", 2)), span)
    grad_previous = select_cells(back_wide, offsets, 1, span, rows, cols, chans)
    merge1_total, merge2_total, head_total, loss = lax.psum(
        (merge1_part, merge2_part, head_part, loss_part), ("gx", "gy")
    )
    return (loss, merge1_total, merge2_total, head_total, grad_current, grad_previous)


def solution(mesh):
    placed = (
        P(None, "gx", "gy", None),
        P(None, "gx", "gy", None),
        P(),
        P(),
        P(),
        P(),
        P(),
        P(),
        P(),
    )
    return jax.shard_map(
        per_device,
        mesh=mesh,
        in_specs=placed,
        out_specs=(P(), P(), P(), P(), P(None, "gx", "gy", None), P(None, "gx", "gy", None)),
        check_vma=False,
    )
```

profile of v0, /device:TPU:1, one launch (start us, length us, event | category | flops | bytes accessed | tf_op | source)
XLA Modules:
  0.0 651.3 jit_solution(12349784794667462889)
XLA Ops:
  7.2 1.0 fusion.156
  8.3 4.6 collective-permute-start
  13.0 5.5 collective-permute-start.1
  20.7 1.0 copy_dynamic-update-slice_fusion.1
  22.9 1.3 collective-permute-start.2
  24.2 1.3 collective-permute-start.3
  25.5 1.4 collective-permute-done.2
  26.9 4.2 collective-permute-done.3
  31.5 1.2 gather_fusion
  32.8 2.1 collective-permute-start.4
  34.9 2.2 collective-permute-start.5
  38.0 2.2 collective-permute-done.5
  40.2 1.3 collective-permute-start.7
  41.5 4.0 collective-permute-start.6
  47.5 1.0 copy-done.1
  50.4 0.9 multiply_convert_fusion.1
  51.3 3.0 collective-permute-start.8
  54.4 1.9 collective-permute-start.9
  56.5 1.0 copy.58
  57.5 2.0 collective-permute-done.9
  59.5 7.7 %collective-permute-start.10 = (bf16[4,10,1,128]{3,2,1,0:T(2,128)(2,1)S(1)}, bf16[4,10,1,128]{3,2,1,0:T(2,128)(2,1)S(1)}, u32[]{:S(2)}, u32[]{:S(2)}) collective-permute-start(bf16[4,10,1,128]{3,2,1,0:T(2,128)(2,1)S(1)} %get-tuple-element.88), channel_id=1, source_target_pairs={{0,1},{1,2},{2,3},{3,4},{4,5},{5,6},{6,7},{7,8},{8,9},{9,10},{10,1... | collective-permute-start | bytes 30728 | tf_op jit(solution)/shard_map/ppermute | solution.py:12
  67.1 1.3 collective-permute-start.11
  68.7 16.9 %collective-permute-done.11 = bf16[4,10,1,128]{3,2,1,0:T(2,128)(2,1)S(1)} collective-permute-done((bf16[4,10,1,128]{3,2,1,0:T(2,128)(2,1)S(1)}, bf16[4,10,1,128]{3,2,1,0:T(2,128)(2,1)S(1)}, u32[]{:S(2)}, u32[]{:S(2)}) %collective-permute-start.11) | collective-permute-done | bytes 10272 | tf_op jit(solution)/shard_map/ppermute | solution.py:15
  89.1 2.8 fusion.33
  91.9 1.2 fusion.5
  93.3 3.1 collective-permute-start.12
  96.4 1.9 collective-permute-start.13
  100.3 1.2 collective-permute-done.13
  101.5 1.3 collective-permute-start.14
  102.8 10.3 %collective-permute-start.15 = (bf16[4,10,1,128]{3,2,1,0:T(2,128)(2,1)S(1)}, bf16[4,10,1,128]{3,2,1,0:T(2,128)(2,1)S(1)}, u32[]{:S(2)}, u32[]{:S(2)}) collective-permute-start(bf16[4,10,1,128]{3,2,1,0:T(2,128)(2,1)S(1)} %get-tuple-element.85), channel_id=1, source_target_pairs={{0,1},{1,2},{2,3},{3,4},{4,5},{5,6},{6,7},{7,8},{8,9},{9,10},{10,1... | collective-permute-start | bytes 30728 | tf_op jit(solution)/shard_map/ppermute | solution.py:12
  116.0 0.9 fusion.18
  116.9 3.3 collective-permute-start.16
  120.3 2.1 collective-permute-start.17
  122.4 0.9 fusion.17
  124.2 0.9 fusion.15
  125.2 0.9 fusion.14
  128.9 0.9 fusion.10
  129.9 1.3 collective-permute-start.18
  131.2 10.6 %collective-permute-start.19 = (bf16[4,10,1,128]{3,2,1,0:T(2,128)(2,1)S(1)}, bf16[4,10,1,128]{3,2,1,0:T(2,128)(2,1)S(1)}, u32[]{:S(2)}, u32[]{:S(2)}) collective-permute-start(bf16[4,10,1,128]{3,2,1,0:T(2,128)(2,1)S(1)} %get-tuple-element.81), channel_id=1, source_target_pairs={{0,1},{1,2},{2,3},{3,4},{4,5},{5,6},{6,7},{7,8},{8,9},{9,10},{10,1... | collective-permute-start | bytes 30728 | tf_op jit(solution)/shard_map/ppermute | solution.py:12
  144.9 4.5 collective-permute-start.20
  150.2 1.9 collective-permute-start.21
  152.3 3.8 collective-permute-done.21
  156.3 10.5 %collective-permute-start.22 = (bf16[4,20,6,128]{3,0,2,1:T(4,128)(2,1)S(1)}, bf16[4,20,6,128]{3,0,2,1:T(4,128)(2,1)S(1)}, u32[]{:S(2)}, u32[]{:S(2)}) collective-permute-start(bf16[4,20,6,128]{3,0,2,1:T(4,128)(2,1)S(1)} %get-tuple-element.42), channel_id=1, source_target_pairs={{0,1},{1,2},{2,3},{3,4},{4,5},{5,6},{6,7},{7,8},{8,9},{9,10},{10,1... | collective-permute-start | bytes 368648 | tf_op jit(solution)/shard_map/ppermute | solution.py:12
  166.8 1.3 collective-permute-start.23
  168.9 136.8 %all-reduce = (f32[]{:T(128)}, f32[128,10]{0,1:T(8,128)}) all-reduce(f32[]{:T(128)S(6)} %div.34, f32[128,10]{0,1:T(8,128)S(1)} %fusion.157), channel_id=1, replica_groups=mesh['gx'=32,'gy'=16] {'gx','gy'}, use_global_device_ids=true, to_apply=%region_2.4 | all-reduce | flops 1281 | bytes 10248 | tf_op jit(solution)/shard_map/psum | solution.py:133
  306.1 1.2 gather_fusion.1
  308.0 333.2 %all-reduce.4.cloned.1.call-done = (f32[3,3,256,128]{3,2,1,0:T(8,128)}, f32[3,3,128,128]{3,2,1,0:T(8,128)}) async-done(((f32[3,3,256,128]{3,2,1,0:T(8,128)}, f32[3,3,128,128]{3,2,1,0:T(8,128)}), (f32[3,3,256,128]{3,2,1,0:T(8,128)}, f32[3,3,128,128]{3,2,1,0:T(8,128)})) %all-reduce.4.cloned.1.call-update) | async-done | bytes 1769488 | tf_op jit(solution)/shard_map/psum | solution.py:133
  641.2 2.4 copy.95
  (185 shorter events, 27.2 us)
Async XLA Ops:
  7.2 81.6 %copy-start = (bf16[128,10]{0,1:T(8,128)(2,1)S(1)}, bf16[128,10]{0,1:T(8,128)(2,1)}, u32[]{:S(2)}) copy-start(bf16[128,10]{0,1:T(8,128)(2,1)} %param.18) | copy-start | bytes 7684
  7.2 15.4 %copy-start.14 = (bf16[4,8,16,128]{3,2,1,0:T(8,128)(2,1)S(1)}, bf16[4,8,16,128]{3,2,1,0:T(8,128)(2,1)}, u32[]{:S(2)}) copy-start(bf16[4,8,16,128]{3,2,1,0:T(8,128)(2,1)} %param.11) | copy-start | bytes 393220
  7.2 15.3 %copy-start.23 = (s32[4,64]{1,0:T(4,128)S(1)}, s32[4,64]{1,0:T(4,128)}, u32[]{:S(2)}) copy-start(s32[4,64]{1,0:T(4,128)} %param.13) | copy-start | bytes 3076
  7.2 634.0 %all-reduce.4.cloned.1.call-start = ((), (), s32[]{:S(2)}) async-start(), calls=%async_computation | async-start | bytes 3538944 | tf_op jit(solution)/shard_map/psum | solution.py:133
  8.2 17.3 %copy-start.25 = (s32[4,2]{0,1:T(2,128)S(1)}, s32[4,2]{0,1:T(2,128)}, u32[]{:S(2)}) copy-start(s32[4,2]{0,1:T(2,128)} %param.12) | copy-start | bytes 100
  8.3 14.3 %collective-permute-start = (bf16[4,6,16,128]{3,0,2,1:T(4,128)(2,1)S(1)}, bf16[4,6,16,128]{3,0,2,1:T(4,128)(2,1)S(1)}, u32[]{:S(2)}, u32[]{:S(2)}) collective-permute-start(bf16[4,6,16,128]{3,0,2,1:T(4,128)(2,1)S(1)} %copy.70), channel_id=1, source_target_pairs={{0,16},{16,32},{32,48},{48,64},{64,80},{80,96},{96,112},{112,128},... | collective-permute-start | bytes 294920 | tf_op jit(solution)/shard_map/ppermute | solution.py:12
  13.0 9.8 %collective-permute-start.1 = (bf16[4,6,16,128]{3,0,2,1:T(4,128)(2,1)S(1)}, bf16[4,6,16,128]{3,0,2,1:T(4,128)(2,1)S(1)}, u32[]{:S(2)}, u32[]{:S(2)}) collective-permute-start(bf16[4,6,16,128]{3,0,2,1:T(4,128)(2,1)S(1)} %copy.71), channel_id=1, source_target_pairs={{16,0},{32,16},{48,32},{64,48},{80,64},{96,80},{112,96},{128,112},... | collective-permute-start | bytes 294920 | tf_op jit(solution)/shard_map/ppermute | solution.py:15
  22.9 4.0 collective-permute-start.2
  24.2 6.9 %collective-permute-start.3 = (bf16[4,20,6,128]{3,0,2,1:T(4,128)(2,1)S(1)}, bf16[4,20,6,128]{3,0,2,1:T(4,128)(2,1)S(1)}, u32[]{:S(2)}, u32[]{:S(2)}) collective-permute-start(bf16[4,20,6,128]{3,0,2,1:T(4,128)(2,1)S(1)} %get-tuple-element.49), channel_id=1, source_target_pairs={{1,0},{2,1},{3,2},{4,3},{5,4},{6,5},{7,6},{8,7},{9,8},{10,9},{11,1... | collective-permute-start | bytes 368648 | tf_op jit(solution)/shard_map/ppermute | solution.py:15
  32.8 5.1 collective-permute-start.4
  34.9 5.2 collective-permute-start.5
  40.2 5.7 collective-permute-start.7
  41.5 4.9 collective-permute-start.6
  47.3 3.0 copy-start.10
  47.4 1.1 copy-start.1
  50.1 6.2 copy-start.24
  50.4 18.1 %copy-start.12 = (bf16[3,3,128,128]{3,2,1,0:T(8,128)(2,1)S(1)}, bf16[3,3,128,128]{3,2,1,0:T(8,128)(2,1)}, u32[]{:S(2)}) copy-start(bf16[3,3,128,128]{3,2,1,0:T(8,128)(2,1)} %param.17) | copy-start | bytes 884740
  51.3 6.1 collective-permute-start.8
  54.4 5.1 collective-permute-start.9
  59.5 9.2 %collective-permute-start.10 = (bf16[4,10,1,128]{3,2,1,0:T(2,128)(2,1)S(1)}, bf16[4,10,1,128]{3,2,1,0:T(2,128)(2,1)S(1)}, u32[]{:S(2)}, u32[]{:S(2)}) collective-permute-start(bf16[4,10,1,128]{3,2,1,0:T(2,128)(2,1)S(1)} %get-tuple-element.88), channel_id=1, source_target_pairs={{0,1},{1,2},{2,3},{3,4},{4,5},{5,6},{6,7},{7,8},{8,9},{9,10},{10,1... | collective-permute-start | bytes 30728 | tf_op jit(solution)/shard_map/ppermute | solution.py:12
  67.1 18.4 %collective-permute-start.11 = (bf16[4,10,1,128]{3,2,1,0:T(2,128)(2,1)S(1)}, bf16[4,10,1,128]{3,2,1,0:T(2,128)(2,1)S(1)}, u32[]{:S(2)}, u32[]{:S(2)}) collective-permute-start(bf16[4,10,1,128]{3,2,1,0:T(2,128)(2,1)S(1)} %get-tuple-element.89), channel_id=1, source_target_pairs={{1,0},{2,1},{3,2},{4,3},{5,4},{6,5},{7,6},{8,7},{9,8},{10,9},{11,1... | collective-permute-start | bytes 30728 | tf_op jit(solution)/shard_map/ppermute | solution.py:15
  68.5 18.7 %copy-start.21 = (bf16[4,8,16,128]{3,2,1,0:T(8,128)(2,1)}, bf16[4,8,16,128]{3,2,1,0:T(8,128)(2,1)S(1)}, u32[]{:S(2)}) copy-start(bf16[4,8,16,128]{3,2,1,0:T(8,128)(2,1)S(1)} %get-tuple-element.98) | copy-start | bytes 393220
  85.9 1.0 copy-start.4
  89.1 4.0 copy-start.9
  91.8 7.0 %copy-start.17 = (bf16[4,8,16,10]{3,2,1,0:T(8,128)(2,1)}, bf16[4,8,16,10]{3,2,1,0:T(8,128)(2,1)S(1)}, u32[]{:S(2)}) copy-start(bf16[4,8,16,10]{3,2,1,0:T(8,128)(2,1)S(1)} %get-tuple-element.50) | copy-start | bytes 30724
  91.9 6.7 %copy-start.7 = (bf16[4,8,16,128]{3,2,1,0:T(8,128)(2,1)S(1)}, bf16[4,8,16,128]{3,2,1,0:T(8,128)(2,1)}, u32[]{:S(2)}) copy-start(bf16[4,8,16,128]{3,2,1,0:T(8,128)(2,1)} %copy-done.6) | copy-start | bytes 393220
  91.9 7.0 %copy-start.3 = (bf16[4,8,16,128]{3,2,1,0:T(8,128)(2,1)S(1)}, bf16[4,8,16,128]{3,2,1,0:T(8,128)(2,1)}, u32[]{:S(2)}) copy-start(bf16[4,8,16,128]{3,2,1,0:T(8,128)(2,1)} %copy-done.2) | copy-start | bytes 393220
  93.0 6.3 copy-start.5
  93.1 6.7 %copy-start.22 = (bf16[4,8,16,128]{3,2,1,0:T(8,128)(2,1)S(1)}, bf16[4,8,16,128]{3,2,1,0:T(8,128)(2,1)}, u32[]{:S(2)}) copy-start(bf16[4,8,16,128]{3,2,1,0:T(8,128)(2,1)} %copy-done.21) | copy-start | bytes 393220
  93.3 7.0 %collective-permute-start.12 = (bf16[4,1,16,128]{3,2,1,0:T(8,128)(2,1)S(1)}, bf16[4,1,16,128]{3,2,1,0:T(8,128)(2,1)S(1)}, u32[]{:S(2)}, u32[]{:S(2)}) collective-permute-start(bf16[4,1,16,128]{3,2,1,0:T(8,128)(2,1)S(1)} %get-tuple-element.96), channel_id=1, source_target_pairs={{0,16},{16,32},{32,48},{48,64},{64,80},{80,96},{96,112},{112,128},... | collective-permute-start | bytes 49160 | tf_op jit(solution)/shard_map/ppermute | solution.py:12
  96.4 5.1 collective-permute-start.13
  99.1 14.1 %copy-start.13 = (bf16[3,3,128,128]{3,2,1,0:T(8,128)(2,1)S(1)}, bf16[3,3,128,128]{3,2,1,0:T(8,128)(2,1)}, u32[]{:S(2)}) copy-start(bf16[3,3,128,128]{3,2,1,0:T(8,128)(2,1)} %param.17) | copy-start | bytes 884740
  100.3 13.9 %copy-start.15 = (f32[9,128,128]{2,1,0:T(8,128)}, f32[9,128,128]{2,1,0:T(8,128)S(1)}, u32[]{:S(2)}) copy-start(f32[9,128,128]{2,1,0:T(8,128)S(1)} %fusion.19) | copy-start | bytes 1769476
  101.5 11.8 %collective-permute-start.14 = (bf16[4,10,1,128]{3,2,1,0:T(2,128)(2,1)S(1)}, bf16[4,10,1,128]{3,2,1,0:T(2,128)(2,1)S(1)}, u32[]{:S(2)}, u32[]{:S(2)}) collective-permute-start(bf16[4,10,1,128]{3,2,1,0:T(2,128)(2,1)S(1)} %get-tuple-element.84), channel_id=1, source_target_pairs={{1,0},{2,1},{3,2},{4,3},{5,4},{6,5},{7,6},{8,7},{9,8},{10,9},{11,1... | collective-permute-start | bytes 30728 | tf_op jit(solution)/shard_map/ppermute | solution.py:15
  102.8 11.2 %collective-permute-start.15 = (bf16[4,10,1,128]{3,2,1,0:T(2,128)(2,1)S(1)}, bf16[4,10,1,128]{3,2,1,0:T(2,128)(2,1)S(1)}, u32[]{:S(2)}, u32[]{:S(2)}) collective-permute-start(bf16[4,10,1,128]{3,2,1,0:T(2,128)(2,1)S(1)} %get-tuple-element.85), channel_id=1, source_target_pairs={{0,1},{1,2},{2,3},{3,4},{4,5},{5,6},{6,7},{7,8},{8,9},{9,10},{10,1... | collective-permute-start | bytes 30728 | tf_op jit(solution)/shard_map/ppermute | solution.py:12
  114.8 1.0 copy-start.26
  116.9 12.9 %collective-permute-start.16 = (bf16[4,1,16,128]{3,2,1,0:T(8,128)(2,1)S(1)}, bf16[4,1,16,128]{3,2,1,0:T(8,128)(2,1)S(1)}, u32[]{:S(2)}, u32[]{:S(2)}) collective-permute-start(bf16[4,1,16,128]{3,2,1,0:T(8,128)(2,1)S(1)} %get-tuple-element.92), channel_id=1, source_target_pairs={{0,16},{16,32},{32,48},{48,64},{64,80},{80,96},{96,112},{112,128},... | collective-permute-start | bytes 49160 | tf_op jit(solution)/shard_map/ppermute | solution.py:12
  120.3 9.5 %collective-permute-start.17 = (bf16[4,1,16,128]{3,2,1,0:T(8,128)(2,1)S(1)}, bf16[4,1,16,128]{3,2,1,0:T(8,128)(2,1)S(1)}, u32[]{:S(2)}, u32[]{:S(2)}) collective-permute-start(bf16[4,1,16,128]{3,2,1,0:T(8,128)(2,1)S(1)} %get-tuple-element.93), channel_id=1, source_target_pairs={{16,0},{32,16},{48,32},{64,48},{80,64},{96,80},{112,96},{128,112},... | collective-permute-start | bytes 49160 | tf_op jit(solution)/shard_map/ppermute | solution.py:15
  125.2 3.7 copy-start.11
  129.9 12.2 %collective-permute-start.18 = (bf16[4,10,1,128]{3,2,1,0:T(2,128)(2,1)S(1)}, bf16[4,10,1,128]{3,2,1,0:T(2,128)(2,1)S(1)}, u32[]{:S(2)}, u32[]{:S(2)}) collective-permute-start(bf16[4,10,1,128]{3,2,1,0:T(2,128)(2,1)S(1)} %get-tuple-element.80), channel_id=1, source_target_pairs={{1,0},{2,1},{3,2},{4,3},{5,4},{6,5},{7,6},{8,7},{9,8},{10,9},{11,1... | collective-permute-start | bytes 30728 | tf_op jit(solution)/shard_map/ppermute | solution.py:15
  131.2 11.5 %collective-permute-start.19 = (bf16[4,10,1,128]{3,2,1,0:T(2,128)(2,1)S(1)}, bf16[4,10,1,128]{3,2,1,0:T(2,128)(2,1)S(1)}, u32[]{:S(2)}, u32[]{:S(2)}) collective-permute-start(bf16[4,10,1,128]{3,2,1,0:T(2,128)(2,1)S(1)} %get-tuple-element.81), channel_id=1, source_target_pairs={{0,1},{1,2},{2,3},{3,4},{4,5},{5,6},{6,7},{7,8},{8,9},{9,10},{10,1... | collective-permute-start | bytes 30728 | tf_op jit(solution)/shard_map/ppermute | solution.py:12
  144.8 23.3 %copy-start.18 = (bf16[4,8,16,10]{3,2,1,0:T(8,128)(2,1)S(1)}, bf16[4,8,16,10]{3,2,1,0:T(8,128)(2,1)}, u32[]{:S(2)}) copy-start(bf16[4,8,16,10]{3,2,1,0:T(8,128)(2,1)} %copy-done.17) | copy-start | bytes 30724
  144.8 23.3 %copy-start.20 = (bf16[512,128]{1,0:T(8,128)(2,1)S(1)}, bf16[512,128]{1,0:T(8,128)(2,1)}, u32[]{:S(2)}) copy-start(bf16[512,128]{1,0:T(8,128)(2,1)} %copy-done.19) | copy-start | bytes 393220
  144.9 7.2 %collective-permute-start.20 = (bf16[4,6,16,128]{3,0,2,1:T(4,128)(2,1)S(1)}, bf16[4,6,16,128]{3,0,2,1:T(4,128)(2,1)S(1)}, u32[]{:S(2)}, u32[]{:S(2)}) collective-permute-start(bf16[4,6,16,128]{3,0,2,1:T(4,128)(2,1)S(1)} %copy.64), channel_id=1, source_target_pairs={{0,16},{16,32},{32,48},{48,64},{64,80},{80,96},{96,112},{112,128},... | collective-permute-start | bytes 294920 | tf_op jit(solution)/shard_map/ppermute | solution.py:12
  150.2 5.9 collective-permute-start.21
  156.3 149.5 %collective-permute-start.22 = (bf16[4,20,6,128]{3,0,2,1:T(4,128)(2,1)S(1)}, bf16[4,20,6,128]{3,0,2,1:T(4,128)(2,1)S(1)}, u32[]{:S(2)}, u32[]{:S(2)}) collective-permute-start(bf16[4,20,6,128]{3,0,2,1:T(4,128)(2,1)S(1)} %get-tuple-element.42), channel_id=1, source_target_pairs={{0,1},{1,2},{2,3},{3,4},{4,5},{5,6},{6,7},{7,8},{8,9},{9,10},{10,1... | collective-permute-start | bytes 368648 | tf_op jit(solution)/shard_map/ppermute | solution.py:12
  166.8 139.0 %collective-permute-start.23 = (bf16[4,20,6,128]{3,0,2,1:T(4,128)(2,1)S(1)}, bf16[4,20,6,128]{3,0,2,1:T(4,128)(2,1)S(1)}, u32[]{:S(2)}, u32[]{:S(2)}) collective-permute-start(bf16[4,20,6,128]{3,0,2,1:T(4,128)(2,1)S(1)} %get-tuple-element.43), channel_id=1, source_target_pairs={{1,0},{2,1},{3,2},{4,3},{5,4},{6,5},{7,6},{8,7},{9,8},{10,9},{11,1... | collective-permute-start | bytes 368648 | tf_op jit(solution)/shard_map/ppermute | solution.py:15
  641.2 2.4 copy-start.16
  (4 other events, 2.8 us)
Sparse Core Ops, SparseCore 0:
  129.9 511.1 all-reduce.3
where the time goes:
time: 652 us; the launch traced here: 651 us
  waiting for transfers between devices  367 us (56%)
  blocking collectives  137 us (21%)
  starting transfers between devices  88.3 us (14%)
  matrix products  20.7 us (3%)
  between operations  16 us (2%)
  local copies, waits for them, and re-layouts  14.2 us (2%)
  other arithmetic  8.69 us (1%)
    psum x1, waiting for transfers between devices, per_device(): lax.psum((merge1_part, merge2_part, head_part, loss_part), ('gx', 'gy'))  333 us
    psum x1, blocking collectives, per_device(): lax.psum((merge1_part, merge2_part, head_part, loss_part), ('gx', 'gy'))  137 us
    ppermute x12, starting transfers between devices, extended(): lax.ppermute(lax.slice_in_dim(block, block.shape[dim] - width, None, axis...  65 us
    ppermute x12, waiting for transfers between devices, extended(): lax.ppermute(lax.slice_in_dim(block, 0, width, axis=dim), axis, backward)  30.3 us
    ppermute x12, starting transfers between devices, extended(): lax.ppermute(lax.slice_in_dim(block, 0, width, axis=dim), axis, backward)  23.3 us
  transfers between devices with their start and end apart: 25, of which 11 were waited for; matrix products, arithmetic and copies ran while one was open for 3% of the time, Pallas kernels for 0%

commit v1 on v0

--- a/solution.py
+++ b/solution.py
@@ -1,7 +1,132 @@
 import jax
 import jax.numpy as jnp
 from jax import lax
+from jax.experimental import pallas as pl
+from jax.experimental.pallas import tpu as pltpu
 from jax.sharding import PartitionSpec as P
+
+
+ROWS = 4096
+HALF, QX, QY, QZ = ROWS // 2, ROWS // 8, ROWS // 32, ROWS // 512
+MESH = pl.DeviceIdType.MESH
+
+
+def place():
+    gx, gy = lax.axis_index("gx"), lax.axis_index("gy")
+    return gx % 2, gy % 4, (gx // 2) % 4, (gy // 4) * 4 + gx // 8
+
+
+def device(core, x, y, z):
+    return {"gx": ((z % 4) * 4 + y) * 2 + core, "gy": (z // 4) * 4 + x}
+
+
+def reduce_kernel(
+    part_ref, out_ref,
+    half_in, half, x_out, x_in, x_own, y_out, y_in, y_own, z_in, z_all,
+    y_all, x_all, c_all, c_send, c_recv, x_send, x_recv, y_send, y_recv, z_send, z_recv,
+):
+    core, x, y, z = place()
+    partner = device(1 - core, x, y, z)
+    xs = [device(core, (x + d) % 4, y, z) for d in range(1, 4)]
+    ys = [device(core, x, (y + d) % 4, z) for d in range(1, 4)]
+    zs = [device(core, x, y, (z + d) % 16) for d in range(1, 16)]
+    barrier = pltpu.get_barrier_semaphore()
+    for peer in [partner, *xs, *ys, *zs]:
+        pl.semaphore_signal(barrier, inc=1, device_id=peer, device_id_type=MESH)
+    pl.semaphore_wait(barrier, 22)
+
+    def copy(src, dst, send, recv, peer):
+        one = pltpu.make_async_remote_copy(
+            src_ref=src, dst_ref=dst, send_sem=send, recv_sem=recv,
+            device_id=peer, device_id_type=MESH,
+        )
+        one.start()
+        return one
+
+    theirs = pl.multiple_of((1 - core) * HALF, HALF)
+    mine = pl.multiple_of(core * HALF, HALF)
+    c = copy(part_ref.at[pl.ds(theirs, HALF)], half_in, c_send.at[0], c_recv.at[0], partner)
+    c.wait()
+    total = part_ref[pl.ds(mine, HALF)] + half_in[...]
+    half[...] = total
+    x_out[...] = total.astype(jnp.bfloat16)
+    cs = [
+        copy(x_out.at[pl.ds(pl.multiple_of(((x + d) % 4) * QX, QX), QX)], x_in.at[d - 1],
+             x_send.at[d - 1], x_recv.at[d - 1], xs[d - 1])
+        for d in range(1, 4)
+    ]
+    total = half[pl.ds(pl.multiple_of(x * QX, QX), QX)]
+    for d in range(3):
+        cs[d].wait()
+        total = total + x_in[d].astype(jnp.float32)
+    x_own[...] = total
+    y_out[...] = total.astype(jnp.bfloat16)
+    cs = [
+        copy(y_out.at[pl.ds(pl.multiple_of(((y + d) % 4) * QY, QY), QY)], y_in.at[d - 1],
+             y_send.at[d - 1], y_recv.at[d - 1], ys[d - 1])
+        for d in range(1, 4)
+    ]
+    total = x_own[pl.ds(pl.multiple_of(y * QY, QY), QY)]
+    for d in range(3):
+        cs[d].wait()
+        total = total + y_in[d].astype(jnp.float32)
+    y_own[...] = total
+    cs = [
+        copy(y_own.at[pl.ds(pl.multiple_of(((z + d) % 16) * QZ, QZ), QZ)], z_in.at[d - 1],
+             z_send.at[d - 1], z_recv.at[d - 1], zs[d - 1])
+        for d in range(1, 16)
+    ]
+    total = y_own[pl.ds(pl.multiple_of(z * QZ, QZ), QZ)]
+    for d in range(15):
+        cs[d].wait()
+        total = total + z_in[d]
+    own = pl.ds(pl.multiple_of(z * QZ, QZ), QZ)
+    z_all[own] = total
+    cs = [
+        copy(z_all.at[own], z_all.at[own], z_send.at[14 + d], z_recv.at[14 + d], zs[d - 1])
+        for d in range(1, 16)
+    ]
+    for one in cs:
+        one.wait()
+    own = pl.ds(pl.multiple_of(y * QY, QY), QY)
+    y_all[own] = z_all[...].astype(jnp.bfloat16)
+    cs = [
+        copy(y_all.at[own], y_all.at[own], y_send.at[2 + d], y_recv.at[2 + d], ys[d - 1])
+        for d in range(1, 4)
+    ]
+    for one in cs:
+        one.wait()
+    own = pl.ds(pl.multiple_of(x * QX, QX), QX)
+    x_all[own] = y_all[...]
+    cs = [
+        copy(x_all.at[own], x_all.at[own], x_send.at[2 + d], x_recv.at[2 + d], xs[d - 1])
+        for d in range(1, 4)
+    ]
+    for one in cs:
+        one.wait()
+    c = copy(x_all, c_all, c_send.at[1], c_recv.at[1], partner)
+    out_ref[pl.ds(mine, HALF)] = x_all[...].astype(jnp.float32)
+    c.wait()
+    out_ref[pl.ds(theirs, HALF)] = c_all[...].astype(jnp.float32)
+
+
+def all_reduce(part):
+    bf, f = jnp.bfloat16, jnp.float32
+    V, D = pltpu.VMEM, pltpu.SemaphoreType.DMA
+    return pl.pallas_call(
+        reduce_kernel,
+        out_shape=jax.ShapeDtypeStruct((ROWS, 128), f),
+        in_specs=[pl.BlockSpec(memory_space=pltpu.VMEM)],
+        out_specs=pl.BlockSpec(memory_space=pltpu.VMEM),
+        scratch_shapes=[
+            V((HALF, 128), f), V((HALF, 128), f), V((HALF, 128), bf), V((3, QX, 128), bf), V((QX, 128), f),
+            V((QX, 128), bf), V((3, QY, 128), bf), V((QY, 128), f), V((15, QZ, 128), f), V((QY, 128), f),
+            V((QX, 128), bf), V((HALF, 128), bf), V((HALF, 128), bf),
+            D((2,)), D((2,)), D((6,)), D((6,)), D((6,)), D((6,)), D((30,)), D((30,)),
+        ],
+        compiler_params=pltpu.CompilerParams(collective_id=1, has_side_effects=True),
+        name="all_reduce",
+    )(part)
 
 
 def extended(block, sides, width):
@@ -130,9 +255,16 @@
     d_aligned = d_stack[..., chans:].astype(jnp.bfloat16)
     back_wide = extended(d_aligned, (("gx", 1), ("gy", 2)), span)
     grad_previous = select_cells(back_wide, offsets, 1, span, rows, cols, chans)
-    merge1_total, merge2_total, head_total, loss = lax.psum(
-        (merge1_part, merge2_part, head_part, loss_part), ("gx", "gy")
-    )
+    part = jnp.concatenate([
+        merge1_part.reshape(-1, chans), merge2_part.reshape(-1, chans),
+        jnp.pad(head_part.T, ((0, 16 - n_cls), (0, 0))),
+        jnp.full((8, chans), loss_part, jnp.float32),
+        jnp.zeros((ROWS - 3480, chans), jnp.float32)])
+    total = all_reduce(part)
+    merge1_total = total[:2304].reshape(3, 3, 2 * chans, chans)
+    merge2_total = total[2304:3456].reshape(3, 3, chans, chans)
+    head_total = total[3456 : 3456 + n_cls].T
+    loss = total[3472, 0]
     return (loss, merge1_total, merge2_total, head_total, grad_current, grad_previous)
 
 

time: 652 us -> 270 us (0.41)
  the two profiles are of different devices: /device:TPU:1 before, /device:TPU:7 now
where the time goes in v1:
time: 270 us; the launch traced here: 269 us
  starting transfers between devices  111 us (41%)
  Pallas kernels  66.2 us (25%)
  waiting for transfers between devices  44.8 us (17%)
  local copies, waits for them, and re-layouts  20.9 us (8%)
  matrix products  14.9 us (6%)
  other arithmetic  8.7 us (3%)
    ppermute x12, starting transfers between devices, extended(): lax.ppermute(lax.slice_in_dim(block, block.shape[dim] - width, None, axis...  87.1 us
    pallas_call x1, Pallas kernels, all_reduce(): pl.pallas_call(reduce_kernel, out_shape=jax.ShapeDtypeStruct((ROWS, 128),...  66.2 us
    ppermute x12, waiting for transfers between devices, extended(): lax.ppermute(lax.slice_in_dim(block, 0, width, axis=dim), axis, backward)  43.1 us
    ppermute x12, starting transfers between devices, extended(): lax.ppermute(lax.slice_in_dim(block, 0, width, axis=dim), axis, backward)  23.9 us
    unnamed x70, local copies, waits for them, and re-layouts  6.7 us
  transfers between devices with their start and end apart: 24, of which 9 were waited for; matrix products, arithmetic and copies ran while one was open for 7% of the time, Pallas kernels for 25%

profile of v1, /device:TPU:7, one launch (start us, length us, event | category | flops | bytes accessed | tf_op | source)
XLA Modules:
  0.0 269.2 jit_solution(725977742364711643)
XLA Ops:
  0.7 1.0 fusion.156
  1.8 3.8 %collective-permute-start = (bf16[4,6,16,128]{3,0,2,1:T(4,128)(2,1)S(1)}, bf16[4,6,16,128]{3,0,2,1:T(4,128)(2,1)S(1)}, u32[]{:S(2)}, u32[]{:S(2)}) collective-permute-start(bf16[4,6,16,128]{3,0,2,1:T(4,128)(2,1)S(1)} %copy.74), channel_id=1, source_target_pairs={{0,16},{16,32},{32,48},{48,64},{64,80},{80,96},{96,112},{112,128},... | collective-permute-start | bytes 294920 | tf_op jit(solution)/shard_map/ppermute | solution.py:137
  5.6 1.9 collective-permute-start.1
  9.8 1.0 copy_dynamic-update-slice_fusion.1
  12.0 8.7 %collective-permute-start.2 = (bf16[4,20,6,128]{3,0,2,1:T(4,128)(2,1)S(1)}, bf16[4,20,6,128]{3,0,2,1:T(4,128)(2,1)S(1)}, u32[]{:S(2)}, u32[]{:S(2)}) collective-permute-start(bf16[4,20,6,128]{3,0,2,1:T(4,128)(2,1)S(1)} %get-tuple-element.44), channel_id=1, source_target_pairs={{0,1},{1,2},{2,3},{3,4},{4,5},{5,6},{6,7},{7,8},{8,9},{9,10},{10,1... | collective-permute-start | bytes 368648 | tf_op jit(solution)/shard_map/ppermute | solution.py:137
  20.7 1.9 collective-permute-start.3
  22.7 9.8 %collective-permute-done.3 = bf16[4,20,6,128]{3,0,2,1:T(4,128)(2,1)S(1)} collective-permute-done((bf16[4,20,6,128]{3,0,2,1:T(4,128)(2,1)S(1)}, bf16[4,20,6,128]{3,0,2,1:T(4,128)(2,1)S(1)}, u32[]{:S(2)}, u32[]{:S(2)}) %collective-permute-start.3) | collective-permute-done | bytes 122912 | tf_op jit(solution)/shard_map/ppermute | solution.py:140
  32.9 1.2 gather_fusion
  34.2 12.9 %collective-permute-start.4 = (bf16[4,1,16,256]{3,0,2,1:T(4,128)(2,1)S(1)}, bf16[4,1,16,256]{3,0,2,1:T(4,128)(2,1)S(1)}, u32[]{:S(2)}, u32[]{:S(2)}) collective-permute-start(bf16[4,1,16,256]{3,0,2,1:T(4,128)(2,1)S(1)} %get-tuple-element.54), channel_id=1, source_target_pairs={{0,16},{16,32},{32,48},{48,64},{64,80},{80,96},{96,112},{112,128},... | collective-permute-start | bytes 98312 | tf_op jit(solution)/shard_map/ppermute | solution.py:137
  47.1 1.9 collective-permute-start.5
  49.8 2.5 collective-permute-done.5
  52.4 1.9 collective-permute-start.7
  54.3 9.4 %collective-permute-start.6 = (bf16[4,10,1,256]{3,0,2,1:T(4,128)(2,1)S(1)}, bf16[4,10,1,256]{3,0,2,1:T(4,128)(2,1)S(1)}, u32[]{:S(2)}, u32[]{:S(2)}) collective-permute-start(bf16[4,10,1,256]{3,0,2,1:T(4,128)(2,1)S(1)} %get-tuple-element.43), channel_id=1, source_target_pairs={{0,1},{1,2},{2,3},{3,4},{4,5},{5,6},{6,7},{7,8},{8,9},{9,10},{10,1... | collective-permute-start | bytes 61448 | tf_op jit(solution)/shard_map/ppermute | solution.py:137
  65.7 1.0 copy-done.2
  68.6 0.9 multiply_convert_fusion.1
  69.5 3.0 %collective-permute-start.8 = (bf16[4,1,16,128]{3,2,1,0:T(8,128)(2,1)S(1)}, bf16[4,1,16,128]{3,2,1,0:T(8,128)(2,1)S(1)}, u32[]{:S(2)}, u32[]{:S(2)}) collective-permute-start(bf16[4,1,16,128]{3,2,1,0:T(8,128)(2,1)S(1)} %get-tuple-element.96), channel_id=1, source_target_pairs={{0,16},{16,32},{32,48},{48,64},{64,80},{80,96},{96,112},{112,128},... | collective-permute-start | bytes 49160 | tf_op jit(solution)/shard_map/ppermute | solution.py:137
  72.6 1.9 collective-permute-start.9
  74.7 1.0 copy.51
  75.7 2.0 collective-permute-done.9
  77.7 10.0 %collective-permute-start.10 = (bf16[4,10,1,128]{3,2,1,0:T(2,128)(2,1)S(1)}, bf16[4,10,1,128]{3,2,1,0:T(2,128)(2,1)S(1)}, u32[]{:S(2)}, u32[]{:S(2)}) collective-permute-start(bf16[4,10,1,128]{3,2,1,0:T(2,128)(2,1)S(1)} %get-tuple-element.84), channel_id=1, source_target_pairs={{0,1},{1,2},{2,3},{3,4},{4,5},{5,6},{6,7},{7,8},{8,9},{9,10},{10,1... | collective-permute-start | bytes 30728 | tf_op jit(solution)/shard_map/ppermute | solution.py:137
  87.6 1.9 collective-permute-start.11
  89.8 8.8 %collective-permute-done.11 = bf16[4,10,1,128]{3,2,1,0:T(2,128)(2,1)S(1)} collective-permute-done((bf16[4,10,1,128]{3,2,1,0:T(2,128)(2,1)S(1)}, bf16[4,10,1,128]{3,2,1,0:T(2,128)(2,1)S(1)}, u32[]{:S(2)}, u32[]{:S(2)}) %collective-permute-start.11) | collective-permute-done | bytes 10272 | tf_op jit(solution)/shard_map/ppermute | solution.py:140
  100.3 0.9 multiply_convert_fusion
  101.5 2.8 %fusion.46 = (f32[]{:T(128)}, bf16[4,8,16,10]{3,2,1,0:T(8,128)(2,1)S(1)}) fusion(f32[4,8,16,10]{3,2,1,0:T(8,128)S(1)} %bitcast.312, f32[4,8,16,10]{3,2,1,0:T(8,128)} %copy.51, u8[4,16,10]{2,1,0:T(8,128)(4,1)S(1)} %fusion.28, f32[512,10]{1,0:T(8,128)S(1)} %copy.67), kind=kLoop, calls=%fused_computation.118 | loop fusion | flops 465919 | bytes 72324 | tf_op jit(solution)/shard_map/jvp()/reduce_sum | solution.py:191
  104.3 1.2 fusion.5
  106.3 3.8 %collective-permute-start.12 = (bf16[4,1,16,128]{3,2,1,0:T(8,128)(2,1)}, bf16[4,1,16,128]{3,2,1,0:T(8,128)(2,1)S(1)}, u32[]{:S(2)}, u32[]{:S(2)}) collective-permute-start(bf16[4,1,16,128]{3,2,1,0:T(8,128)(2,1)} %get-tuple-element.92), channel_id=1, source_target_pairs={{0,16},{16,32},{32,48},{48,64},{64,80},{80,96},{96,112},{112,128},... | collective-permute-start | bytes 49160 | tf_op jit(solution)/shard_map/ppermute | solution.py:137
  110.1 1.9 collective-permute-start.13
  113.9 0.8 copy-done.18
  115.7 1.9 collective-permute-start.14
  117.6 9.4 %collective-permute-start.15 = (bf16[4,10,1,128]{3,2,1,0:T(2,128)(2,1)S(1)}, bf16[4,10,1,128]{3,2,1,0:T(2,128)(2,1)S(1)}, u32[]{:S(2)}, u32[]{:S(2)}) collective-permute-start(bf16[4,10,1,128]{3,2,1,0:T(2,128)(2,1)S(1)} %get-tuple-element.81), channel_id=1, source_target_pairs={{0,1},{1,2},{2,3},{3,4},{4,5},{5,6},{6,7},{7,8},{8,9},{9,10},{10,1... | collective-permute-start | bytes 30728 | tf_op jit(solution)/shard_map/ppermute | solution.py:137
  130.2 4.8 %collective-permute-start.16 = (bf16[4,1,16,128]{3,2,1,0:T(8,128)(2,1)S(1)}, bf16[4,1,16,128]{3,2,1,0:T(8,128)(2,1)S(1)}, u32[]{:S(2)}, u32[]{:S(2)}) collective-permute-start(bf16[4,1,16,128]{3,2,1,0:T(8,128)(2,1)S(1)} %get-tuple-element.88), channel_id=1, source_target_pairs={{0,16},{16,32},{32,48},{48,64},{64,80},{80,96},{96,112},{112,128},... | collective-permute-start | bytes 49160 | tf_op jit(solution)/shard_map/ppermute | solution.py:137
  135.0 2.1 collective-permute-start.17
  139.4 1.0 copy-done.19
  140.5 1.3 copy-done.1
  141.8 66.2 %all_reduce.1 = f32[4096,128]{1,0:T(8,128)} custom-call(f32[4096,128]{1,0:T(8,128)} %copy-done.1), custom_call_target="tpu_custom_call" | custom-call | tf_op jit(solution)/shard_map/all_reduce/pallas_call | solution.py:116
  208.0 1.2 slice.378
  209.2 1.9 slice.380
  211.1 2.4 slice.379
  213.5 2.6 collective-permute-start.18
  216.1 8.7 %collective-permute-start.19 = (bf16[4,10,1,128]{3,2,1,0:T(2,128)(2,1)S(1)}, bf16[4,10,1,128]{3,2,1,0:T(2,128)(2,1)S(1)}, u32[]{:S(2)}, u32[]{:S(2)}) collective-permute-start(bf16[4,10,1,128]{3,2,1,0:T(2,128)(2,1)S(1)} %get-tuple-element.77), channel_id=1, source_target_pairs={{0,1},{1,2},{2,3},{3,4},{4,5},{5,6},{6,7},{7,8},{8,9},{9,10},{10,1... | collective-permute-start | bytes 30728 | tf_op jit(solution)/shard_map/ppermute | solution.py:137
  227.9 2.8 %collective-permute-start.20 = (bf16[4,6,16,128]{3,0,2,1:T(4,128)(2,1)S(1)}, bf16[4,6,16,128]{3,0,2,1:T(4,128)(2,1)S(1)}, u32[]{:S(2)}, u32[]{:S(2)}) collective-permute-start(bf16[4,6,16,128]{3,0,2,1:T(4,128)(2,1)S(1)} %copy.68), channel_id=1, source_target_pairs={{0,16},{16,32},{32,48},{48,64},{64,80},{80,96},{96,112},{112,128},... | collective-permute-start | bytes 294920 | tf_op jit(solution)/shard_map/ppermute | solution.py:137
  231.5 1.9 collective-permute-start.21
  233.6 3.8 %collective-permute-done.21 = bf16[4,6,16,128]{3,0,2,1:T(4,128)(2,1)S(1)} collective-permute-done((bf16[4,6,16,128]{3,0,2,1:T(4,128)(2,1)S(1)}, bf16[4,6,16,128]{3,0,2,1:T(4,128)(2,1)S(1)}, u32[]{:S(2)}, u32[]{:S(2)}) %collective-permute-start.21) | collective-permute-done | bytes 98336 | tf_op jit(solution)/shard_map/ppermute | solution.py:140
  237.5 10.0 %collective-permute-start.22 = (bf16[4,20,6,128]{3,0,2,1:T(4,128)(2,1)S(1)}, bf16[4,20,6,128]{3,0,2,1:T(4,128)(2,1)S(1)}, u32[]{:S(2)}, u32[]{:S(2)}) collective-permute-start(bf16[4,20,6,128]{3,0,2,1:T(4,128)(2,1)S(1)} %get-tuple-element.38), channel_id=1, source_target_pairs={{0,1},{1,2},{2,3},{3,4},{4,5},{5,6},{6,7},{7,8},{8,9},{9,10},{10,1... | collective-permute-start | bytes 368648 | tf_op jit(solution)/shard_map/ppermute | solution.py:137
  247.5 1.9 collective-permute-start.23
  249.5 1.3 slice_bitcast_fusion
  250.8 16.2 %collective-permute-done.23 = bf16[4,20,6,128]{3,0,2,1:T(4,128)(2,1)S(1)} collective-permute-done((bf16[4,20,6,128]{3,0,2,1:T(4,128)(2,1)S(1)}, bf16[4,20,6,128]{3,0,2,1:T(4,128)(2,1)S(1)}, u32[]{:S(2)}, u32[]{:S(2)}) %collective-permute-start.23) | collective-permute-done | bytes 122912 | tf_op jit(solution)/shard_map/ppermute | solution.py:140
  267.3 1.2 gather_fusion.1
  (191 shorter events, 24.3 us)
Async XLA Ops:
  0.6 100.5 %copy-start = (bf16[128,10]{0,1:T(8,128)(2,1)S(1)}, bf16[128,10]{0,1:T(8,128)(2,1)}, u32[]{:S(2)}) copy-start(bf16[128,10]{0,1:T(8,128)(2,1)} %param.18) | copy-start | bytes 7684
  0.6 11.1 %copy-start.17 = (bf16[4,8,16,128]{3,2,1,0:T(8,128)(2,1)S(1)}, bf16[4,8,16,128]{3,2,1,0:T(8,128)(2,1)}, u32[]{:S(2)}) copy-start(bf16[4,8,16,128]{3,2,1,0:T(8,128)(2,1)} %param.11) | copy-start | bytes 393220
  0.7 10.9 %copy-start.24 = (s32[4,64]{1,0:T(4,128)S(1)}, s32[4,64]{1,0:T(4,128)}, u32[]{:S(2)}) copy-start(s32[4,64]{1,0:T(4,128)} %param.13) | copy-start | bytes 3076
  1.7 21.0 %copy-start.26 = (s32[4,2]{0,1:T(2,128)S(1)}, s32[4,2]{0,1:T(2,128)}, u32[]{:S(2)}) copy-start(s32[4,2]{0,1:T(2,128)} %param.12) | copy-start | bytes 100
  1.8 9.9 %collective-permute-start = (bf16[4,6,16,128]{3,0,2,1:T(4,128)(2,1)S(1)}, bf16[4,6,16,128]{3,0,2,1:T(4,128)(2,1)S(1)}, u32[]{:S(2)}, u32[]{:S(2)}) collective-permute-start(bf16[4,6,16,128]{3,0,2,1:T(4,128)(2,1)S(1)} %copy.74), channel_id=1, source_target_pairs={{0,16},{16,32},{32,48},{48,64},{64,80},{80,96},{96,112},{112,128},... | collective-permute-start | bytes 294920 | tf_op jit(solution)/shard_map/ppermute | solution.py:137
  5.6 6.2 %collective-permute-start.1 = (bf16[4,6,16,128]{3,0,2,1:T(4,128)(2,1)S(1)}, bf16[4,6,16,128]{3,0,2,1:T(4,128)(2,1)S(1)}, u32[]{:S(2)}, u32[]{:S(2)}) collective-permute-start(bf16[4,6,16,128]{3,0,2,1:T(4,128)(2,1)S(1)} %copy.75), channel_id=1, source_target_pairs={{16,0},{32,16},{48,32},{64,48},{80,64},{96,80},{112,96},{128,112},... | collective-permute-start | bytes 294920 | tf_op jit(solution)/shard_map/ppermute | solution.py:140
  12.0 10.7 %collective-permute-start.2 = (bf16[4,20,6,128]{3,0,2,1:T(4,128)(2,1)S(1)}, bf16[4,20,6,128]{3,0,2,1:T(4,128)(2,1)S(1)}, u32[]{:S(2)}, u32[]{:S(2)}) collective-permute-start(bf16[4,20,6,128]{3,0,2,1:T(4,128)(2,1)S(1)} %get-tuple-element.44), channel_id=1, source_target_pairs={{0,1},{1,2},{2,3},{3,4},{4,5},{5,6},{6,7},{7,8},{8,9},{9,10},{10,1... | collective-permute-start | bytes 368648 | tf_op jit(solution)/shard_map/ppermute | solution.py:137
  20.7 11.7 %collective-permute-start.3 = (bf16[4,20,6,128]{3,0,2,1:T(4,128)(2,1)S(1)}, bf16[4,20,6,128]{3,0,2,1:T(4,128)(2,1)S(1)}, u32[]{:S(2)}, u32[]{:S(2)}) collective-permute-start(bf16[4,20,6,128]{3,0,2,1:T(4,128)(2,1)S(1)} %get-tuple-element.45), channel_id=1, source_target_pairs={{1,0},{2,1},{3,2},{4,3},{5,4},{6,5},{7,6},{8,7},{9,8},{10,9},{11,1... | collective-permute-start | bytes 368648 | tf_op jit(solution)/shard_map/ppermute | solution.py:140
  34.2 15.6 %collective-permute-start.4 = (bf16[4,1,16,256]{3,0,2,1:T(4,128)(2,1)S(1)}, bf16[4,1,16,256]{3,0,2,1:T(4,128)(2,1)S(1)}, u32[]{:S(2)}, u32[]{:S(2)}) collective-permute-start(bf16[4,1,16,256]{3,0,2,1:T(4,128)(2,1)S(1)} %get-tuple-element.54), channel_id=1, source_target_pairs={{0,16},{16,32},{32,48},{48,64},{64,80},{80,96},{96,112},{112,128},... | collective-permute-start | bytes 98312 | tf_op jit(solution)/shard_map/ppermute | solution.py:137
  47.1 5.2 %collective-permute-start.5 = (bf16[4,1,16,256]{3,0,2,1:T(4,128)(2,1)S(1)}, bf16[4,1,16,256]{3,0,2,1:T(4,128)(2,1)S(1)}, u32[]{:S(2)}, u32[]{:S(2)}) collective-permute-start(bf16[4,1,16,256]{3,0,2,1:T(4,128)(2,1)S(1)} %get-tuple-element.55), channel_id=1, source_target_pairs={{16,0},{32,16},{48,32},{64,48},{80,64},{96,80},{112,96},{128,112},... | collective-permute-start | bytes 98312 | tf_op jit(solution)/shard_map/ppermute | solution.py:140
  52.4 11.8 %collective-permute-start.7 = (bf16[4,10,1,256]{3,0,2,1:T(4,128)(2,1)S(1)}, bf16[4,10,1,256]{3,0,2,1:T(4,128)(2,1)S(1)}, u32[]{:S(2)}, u32[]{:S(2)}) collective-permute-start(bf16[4,10,1,256]{3,0,2,1:T(4,128)(2,1)S(1)} %get-tuple-element.42), channel_id=1, source_target_pairs={{1,0},{2,1},{3,2},{4,3},{5,4},{6,5},{7,6},{8,7},{9,8},{10,9},{11,1... | collective-permute-start | bytes 61448 | tf_op jit(solution)/shard_map/ppermute | solution.py:140
  54.3 10.3 %collective-permute-start.6 = (bf16[4,10,1,256]{3,0,2,1:T(4,128)(2,1)S(1)}, bf16[4,10,1,256]{3,0,2,1:T(4,128)(2,1)S(1)}, u32[]{:S(2)}, u32[]{:S(2)}) collective-permute-start(bf16[4,10,1,256]{3,0,2,1:T(4,128)(2,1)S(1)} %get-tuple-element.43), channel_id=1, source_target_pairs={{0,1},{1,2},{2,3},{3,4},{4,5},{5,6},{6,7},{7,8},{8,9},{9,10},{10,1... | collective-permute-start | bytes 61448 | tf_op jit(solution)/shard_map/ppermute | solution.py:137
  65.5 3.0 %copy-start.13 = (bf16[4,8,16,256]{3,2,1,0:T(8,128)(2,1)}, bf16[4,8,16,256]{3,2,1,0:T(8,128)(2,1)S(1)}, u32[]{:S(2)}) copy-start(bf16[4,8,16,256]{3,2,1,0:T(8,128)(2,1)S(1)} %copy.59) | copy-start | bytes 786436
  65.6 1.1 copy-start.2
  68.3 6.2 %copy-start.25 = (s32[4,64]{1,0:T(4,128)S(1)}, s32[4,64]{1,0:T(4,128)}, u32[]{:S(2)}) copy-start(s32[4,64]{1,0:T(4,128)} %param.15) | copy-start | bytes 3076
  68.6 21.0 %copy-start.15 = (bf16[3,3,128,128]{3,2,1,0:T(8,128)(2,1)S(1)}, bf16[3,3,128,128]{3,2,1,0:T(8,128)(2,1)}, u32[]{:S(2)}) copy-start(bf16[3,3,128,128]{3,2,1,0:T(8,128)(2,1)} %param.17) | copy-start | bytes 884740
  69.5 6.1 %collective-permute-start.8 = (bf16[4,1,16,128]{3,2,1,0:T(8,128)(2,1)S(1)}, bf16[4,1,16,128]{3,2,1,0:T(8,128)(2,1)S(1)}, u32[]{:S(2)}, u32[]{:S(2)}) collective-permute-start(bf16[4,1,16,128]{3,2,1,0:T(8,128)(2,1)S(1)} %get-tuple-element.96), channel_id=1, source_target_pairs={{0,16},{16,32},{32,48},{48,64},{64,80},{80,96},{96,112},{112,128},... | collective-permute-start | bytes 49160 | tf_op jit(solution)/shard_map/ppermute | solution.py:137
  72.6 5.1 %collective-permute-start.9 = (bf16[4,1,16,128]{3,2,1,0:T(8,128)(2,1)S(1)}, bf16[4,1,16,128]{3,2,1,0:T(8,128)(2,1)S(1)}, u32[]{:S(2)}, u32[]{:S(2)}) collective-permute-start(bf16[4,1,16,128]{3,2,1,0:T(8,128)(2,1)S(1)} %get-tuple-element.97), channel_id=1, source_target_pairs={{16,0},{32,16},{48,32},{64,48},{80,64},{96,80},{112,96},{128,112},... | collective-permute-start | bytes 49160 | tf_op jit(solution)/shard_map/ppermute | solution.py:140
  77.7 12.1 %collective-permute-start.10 = (bf16[4,10,1,128]{3,2,1,0:T(2,128)(2,1)S(1)}, bf16[4,10,1,128]{3,2,1,0:T(2,128)(2,1)S(1)}, u32[]{:S(2)}, u32[]{:S(2)}) collective-permute-start(bf16[4,10,1,128]{3,2,1,0:T(2,128)(2,1)S(1)} %get-tuple-element.84), channel_id=1, source_target_pairs={{0,1},{1,2},{2,3},{3,4},{4,5},{5,6},{6,7},{7,8},{8,9},{9,10},{10,1... | collective-permute-start | bytes 30728 | tf_op jit(solution)/shard_map/ppermute | solution.py:137
  87.6 11.0 %collective-permute-start.11 = (bf16[4,10,1,128]{3,2,1,0:T(2,128)(2,1)S(1)}, bf16[4,10,1,128]{3,2,1,0:T(2,128)(2,1)S(1)}, u32[]{:S(2)}, u32[]{:S(2)}) collective-permute-start(bf16[4,10,1,128]{3,2,1,0:T(2,128)(2,1)S(1)} %get-tuple-element.85), channel_id=1, source_target_pairs={{1,0},{2,1},{3,2},{4,3},{5,4},{6,5},{7,6},{8,7},{9,8},{10,9},{11,1... | collective-permute-start | bytes 30728 | tf_op jit(solution)/shard_map/ppermute | solution.py:140
  89.6 10.7 %copy-start.20 = (bf16[4,8,16,128]{3,2,1,0:T(8,128)(2,1)}, bf16[4,8,16,128]{3,2,1,0:T(8,128)(2,1)S(1)}, u32[]{:S(2)}) copy-start(bf16[4,8,16,128]{3,2,1,0:T(8,128)(2,1)S(1)} %get-tuple-element.94) | copy-start | bytes 393220
  98.8 1.2 copy-start.3
  98.9 0.9 copy-start.7
  101.2 3.1 %copy-start.22 = (bf16[512,128]{1,0:T(8,128)(2,1)}, bf16[512,128]{1,0:T(8,128)(2,1)S(1)}, u32[]{:S(2)}) copy-start(bf16[512,128]{1,0:T(8,128)(2,1)S(1)} %get-tuple-element.104) | copy-start | bytes 393220
  101.5 3.9 %copy-start.12 = (bf16[4,8,16,128]{3,2,1,0:T(8,128)(2,1)S(1)}, bf16[4,8,16,128]{3,2,1,0:T(8,128)(2,1)}, u32[]{:S(2)}) copy-start(bf16[4,8,16,128]{3,2,1,0:T(8,128)(2,1)} %copy-done.11) | copy-start | bytes 393220
  104.2 8.0 %copy-start.10 = (bf16[4,8,16,128]{3,2,1,0:T(8,128)(2,1)S(1)}, bf16[4,8,16,128]{3,2,1,0:T(8,128)(2,1)}, u32[]{:S(2)}) copy-start(bf16[4,8,16,128]{3,2,1,0:T(8,128)(2,1)} %copy-done.9) | copy-start | bytes 393220
  104.2 8.2 %copy-start.6 = (bf16[4,8,16,128]{3,2,1,0:T(8,128)(2,1)S(1)}, bf16[4,8,16,128]{3,2,1,0:T(8,128)(2,1)}, u32[]{:S(2)}) copy-start(bf16[4,8,16,128]{3,2,1,0:T(8,128)(2,1)} %copy-done.5) | copy-start | bytes 393220
  105.4 7.5 %copy-start.8 = (bf16[4,8,16,128]{3,2,1,0:T(8,128)(2,1)S(1)}, bf16[4,8,16,128]{3,2,1,0:T(8,128)(2,1)}, u32[]{:S(2)}) copy-start(bf16[4,8,16,128]{3,2,1,0:T(8,128)(2,1)} %copy-done.7) | copy-start | bytes 393220
  105.4 7.8 %copy-start.4 = (bf16[4,8,16,128]{3,2,1,0:T(8,128)(2,1)S(1)}, bf16[4,8,16,128]{3,2,1,0:T(8,128)(2,1)}, u32[]{:S(2)}) copy-start(bf16[4,8,16,128]{3,2,1,0:T(8,128)(2,1)} %copy-done.3) | copy-start | bytes 393220
  105.4 8.0 %copy-start.21 = (bf16[4,8,16,128]{3,2,1,0:T(8,128)(2,1)S(1)}, bf16[4,8,16,128]{3,2,1,0:T(8,128)(2,1)}, u32[]{:S(2)}) copy-start(bf16[4,8,16,128]{3,2,1,0:T(8,128)(2,1)} %copy-done.20) | copy-start | bytes 393220
  106.3 9.3 %collective-permute-start.12 = (bf16[4,1,16,128]{3,2,1,0:T(8,128)(2,1)}, bf16[4,1,16,128]{3,2,1,0:T(8,128)(2,1)S(1)}, u32[]{:S(2)}, u32[]{:S(2)}) collective-permute-start(bf16[4,1,16,128]{3,2,1,0:T(8,128)(2,1)} %get-tuple-element.92), channel_id=1, source_target_pairs={{0,16},{16,32},{32,48},{48,64},{64,80},{80,96},{96,112},{112,128},... | collective-permute-start | bytes 49160 | tf_op jit(solution)/shard_map/ppermute | solution.py:137
  110.1 5.6 %collective-permute-start.13 = (bf16[4,1,16,128]{3,2,1,0:T(8,128)(2,1)}, bf16[4,1,16,128]{3,2,1,0:T(8,128)(2,1)S(1)}, u32[]{:S(2)}, u32[]{:S(2)}) collective-permute-start(bf16[4,1,16,128]{3,2,1,0:T(8,128)(2,1)} %get-tuple-element.93), channel_id=1, source_target_pairs={{16,0},{32,16},{48,32},{64,48},{80,64},{96,80},{112,96},{128,112},... | collective-permute-start | bytes 49160 | tf_op jit(solution)/shard_map/ppermute | solution.py:140
  112.2 2.5 copy-start.23
  113.0 14.0 %copy-start.16 = (bf16[3,3,128,128]{3,2,1,0:T(8,128)(2,1)S(1)}, bf16[3,3,128,128]{3,2,1,0:T(8,128)(2,1)}, u32[]{:S(2)}) copy-start(bf16[3,3,128,128]{3,2,1,0:T(8,128)(2,1)} %param.17) | copy-start | bytes 884740
  115.7 11.5 %collective-permute-start.14 = (bf16[4,10,1,128]{3,2,1,0:T(2,128)(2,1)S(1)}, bf16[4,10,1,128]{3,2,1,0:T(2,128)(2,1)S(1)}, u32[]{:S(2)}, u32[]{:S(2)}) collective-permute-start(bf16[4,10,1,128]{3,2,1,0:T(2,128)(2,1)S(1)} %get-tuple-element.80), channel_id=1, source_target_pairs={{1,0},{2,1},{3,2},{4,3},{5,4},{6,5},{7,6},{8,7},{9,8},{10,9},{11,1... | collective-permute-start | bytes 30728 | tf_op jit(solution)/shard_map/ppermute | solution.py:140
  117.6 10.3 %collective-permute-start.15 = (bf16[4,10,1,128]{3,2,1,0:T(2,128)(2,1)S(1)}, bf16[4,10,1,128]{3,2,1,0:T(2,128)(2,1)S(1)}, u32[]{:S(2)}, u32[]{:S(2)}) collective-permute-start(bf16[4,10,1,128]{3,2,1,0:T(2,128)(2,1)S(1)} %get-tuple-element.81), channel_id=1, source_target_pairs={{0,1},{1,2},{2,3},{3,4},{4,5},{5,6},{6,7},{7,8},{8,9},{9,10},{10,1... | collective-permute-start | bytes 30728 | tf_op jit(solution)/shard_map/ppermute | solution.py:137
  128.7 1.0 copy-start.27
  130.2 83.3 %collective-permute-start.16 = (bf16[4,1,16,128]{3,2,1,0:T(8,128)(2,1)S(1)}, bf16[4,1,16,128]{3,2,1,0:T(8,128)(2,1)S(1)}, u32[]{:S(2)}, u32[]{:S(2)}) collective-permute-start(bf16[4,1,16,128]{3,2,1,0:T(8,128)(2,1)S(1)} %get-tuple-element.88), channel_id=1, source_target_pairs={{0,16},{16,32},{32,48},{48,64},{64,80},{80,96},{96,112},{112,128},... | collective-permute-start | bytes 49160 | tf_op jit(solution)/shard_map/ppermute | solution.py:137
  135.0 78.5 %collective-permute-start.17 = (bf16[4,1,16,128]{3,2,1,0:T(8,128)(2,1)S(1)}, bf16[4,1,16,128]{3,2,1,0:T(8,128)(2,1)S(1)}, u32[]{:S(2)}, u32[]{:S(2)}) collective-permute-start(bf16[4,1,16,128]{3,2,1,0:T(8,128)(2,1)S(1)} %get-tuple-element.89), channel_id=1, source_target_pairs={{16,0},{32,16},{48,32},{64,48},{80,64},{96,80},{112,96},{128,112},... | collective-permute-start | bytes 49160 | tf_op jit(solution)/shard_map/ppermute | solution.py:140
  137.9 1.1 copy-start.14
  139.3 1.1 copy-start.19
  140.5 1.3 copy-start.1
  213.5 11.6 %collective-permute-start.18 = (bf16[4,10,1,128]{3,2,1,0:T(2,128)(2,1)S(1)}, bf16[4,10,1,128]{3,2,1,0:T(2,128)(2,1)S(1)}, u32[]{:S(2)}, u32[]{:S(2)}) collective-permute-start(bf16[4,10,1,128]{3,2,1,0:T(2,128)(2,1)S(1)} %get-tuple-element.76), channel_id=1, source_target_pairs={{1,0},{2,1},{3,2},{4,3},{5,4},{6,5},{7,6},{8,7},{9,8},{10,9},{11,1... | collective-permute-start | bytes 30728 | tf_op jit(solution)/shard_map/ppermute | solution.py:140
  216.1 9.6 %collective-permute-start.19 = (bf16[4,10,1,128]{3,2,1,0:T(2,128)(2,1)S(1)}, bf16[4,10,1,128]{3,2,1,0:T(2,128)(2,1)S(1)}, u32[]{:S(2)}, u32[]{:S(2)}) collective-permute-start(bf16[4,10,1,128]{3,2,1,0:T(2,128)(2,1)S(1)} %get-tuple-element.77), channel_id=1, source_target_pairs={{0,1},{1,2},{2,3},{3,4},{4,5},{5,6},{6,7},{7,8},{8,9},{9,10},{10,1... | collective-permute-start | bytes 30728 | tf_op jit(solution)/shard_map/ppermute | solution.py:137
  227.9 5.5 %collective-permute-start.20 = (bf16[4,6,16,128]{3,0,2,1:T(4,128)(2,1)S(1)}, bf16[4,6,16,128]{3,0,2,1:T(4,128)(2,1)S(1)}, u32[]{:S(2)}, u32[]{:S(2)}) collective-permute-start(bf16[4,6,16,128]{3,0,2,1:T(4,128)(2,1)S(1)} %copy.68), channel_id=1, source_target_pairs={{0,16},{16,32},{32,48},{48,64},{64,80},{80,96},{96,112},{112,128},... | collective-permute-start | bytes 294920 | tf_op jit(solution)/shard_map/ppermute | solution.py:137
  231.5 5.9 %collective-permute-start.21 = (bf16[4,6,16,128]{3,0,2,1:T(4,128)(2,1)S(1)}, bf16[4,6,16,128]{3,0,2,1:T(4,128)(2,1)S(1)}, u32[]{:S(2)}, u32[]{:S(2)}) collective-permute-start(bf16[4,6,16,128]{3,0,2,1:T(4,128)(2,1)S(1)} %copy.70), channel_id=1, source_target_pairs={{16,0},{32,16},{48,32},{64,48},{80,64},{96,80},{112,96},{128,112},... | collective-permute-start | bytes 294920 | tf_op jit(solution)/shard_map/ppermute | solution.py:140
  237.5 13.2 %collective-permute-start.22 = (bf16[4,20,6,128]{3,0,2,1:T(4,128)(2,1)S(1)}, bf16[4,20,6,128]{3,0,2,1:T(4,128)(2,1)S(1)}, u32[]{:S(2)}, u32[]{:S(2)}) collective-permute-start(bf16[4,20,6,128]{3,0,2,1:T(4,128)(2,1)S(1)} %get-tuple-element.38), channel_id=1, source_target_pairs={{0,1},{1,2},{2,3},{3,4},{4,5},{5,6},{6,7},{7,8},{8,9},{9,10},{10,1... | collective-permute-start | bytes 368648 | tf_op jit(solution)/shard_map/ppermute | solution.py:137
  247.5 19.4 %collective-permute-start.23 = (bf16[4,20,6,128]{3,0,2,1:T(4,128)(2,1)S(1)}, bf16[4,20,6,128]{3,0,2,1:T(4,128)(2,1)S(1)}, u32[]{:S(2)}, u32[]{:S(2)}) collective-permute-start(bf16[4,20,6,128]{3,0,2,1:T(4,128)(2,1)S(1)} %get-tuple-element.39), channel_id=1, source_target_pairs={{1,0},{2,1},{3,2},{4,3},{5,4},{6,5},{7,6},{8,7},{9,8},{10,9},{11,1... | collective-permute-start | bytes 368648 | tf_op jit(solution)/shard_map/ppermute | solution.py:140
  (4 other events, 2.9 us)

commit v2 on v1

v2 whole, which is shorter than its diff:
```python
import jax
import jax.numpy as jnp
from jax import lax
from jax.experimental import pallas as pl
from jax.experimental.pallas import tpu as pltpu
from jax.sharding import PartitionSpec as P

FAR = 1e9
ROWS = 4096
HALF, QX, QY, QZ = ROWS // 2, ROWS // 8, ROWS // 32, ROWS // 512
MESH = pl.DeviceIdType.MESH


def place():
    gx, gy = lax.axis_index("gx"), lax.axis_index("gy")
    return gx % 2, gy % 4, (gx // 2) % 4, (gy // 4) * 4 + gx // 8


def device(core, x, y, z):
    return {"gx": ((z % 4) * 4 + y) * 2 + core, "gy": (z // 4) * 4 + x}
AROUND = tuple((r, c) for r in (-1, 0, 1) for c in (-1, 0, 1) if r or c)
VM = pl.BlockSpec(memory_space=pltpu.VMEM)


def around():
    gx, gy = lax.axis_index("gx"), lax.axis_index("gy")
    return [{"gx": (gx + r + 32) % 32, "gy": (gy + c + 16) % 16} for r, c in AROUND]


def exchange(src, dst, high, wide, send, recv, base):
    copies = []
    for n, ((r, c), peer) in enumerate(zip(AROUND, around())):
        r0, r1, nr = {1: (8 - high, 0, high), -1: (0, high + 8, high), 0: (0, high, 8)}[r]
        c0, c1, nc = {1: (8 - wide, 0, wide), -1: (0, wide + 8, wide), 0: (0, wide, 8)}[c]
        one = pltpu.make_async_remote_copy(
            src_ref=src.at[r0 : r0 + nr, c0 : c0 + nc], dst_ref=dst.at[r1 : r1 + nr, c1 : c1 + nc],
            send_sem=send.at[base + n], recv_sem=recv.at[base + n], device_id=peer, device_id_type=MESH,
        )
        one.start()
        copies.append(one)
    dst[high : high + 8, wide : wide + 8] = src[...]
    return copies


def greet():
    barrier = pltpu.get_barrier_semaphore()
    for peer in around():
        pl.semaphore_signal(barrier, inc=1, device_id=peer, device_id_type=MESH)
    pl.semaphore_wait(barrier, 8)


def inputs_kernel(cur_ref, prev_ref, obj_ref, cur_wide, prev_wide, near_ref, send, recv):
    greet()
    copies = exchange(prev_ref, prev_wide, 8, 4, send, recv, 0)
    copies += exchange(cur_ref, cur_wide, 2, 1, send, recv, 8)
    lane = lax.broadcasted_iota(jnp.int32, (1, 512), 1)
    scene = lane % 4
    row = (lane // 64 + lax.axis_index("gx") * 8).astype(jnp.float32)
    col = ((lane // 4) % 16 + lax.axis_index("gy") * 16).astype(jnp.float32)

    def of_scene(first):
        value = jnp.broadcast_to(obj_ref[:, first : first + 1], (64, 512))
        for s in range(1, 4):
            value = jnp.where(scene == s, obj_ref[:, first + s : first + s + 1], value)
        return value

    dr = row - of_scene(0)
    dc = col - of_scene(4)
    kind = of_scene(8)
    square = dr * dr + dc * dc
    for k in range(16):
        near_ref[k : k + 1] = jnp.min(jnp.where(kind == k, square, FAR), axis=0, keepdims=True)
    for one in copies:
        one.wait()


def exchange_inputs(cur, prev, obj):
    shape, D = jax.ShapeDtypeStruct, pltpu.SemaphoreType.DMA
    return pl.pallas_call(
        inputs_kernel,
        out_shape=(
            shape((12, 10, 8, 128), jnp.bfloat16), shape((24, 16, 8, 128), jnp.bfloat16),
            shape((16, 512), jnp.float32),
        ),
        in_specs=[VM] * 3, out_specs=(VM,) * 3,
        scratch_shapes=[D((16,)), D((16,))],
        compiler_params=pltpu.CompilerParams(collective_id=2, has_side_effects=True),
        name="exchange_inputs",
    )(cur, prev, obj)


def border_kernel(src_ref, dst_ref, send, recv):
    greet()
    for one in exchange(src_ref, dst_ref, 2, 1, send, recv, 0):
        one.wait()


def exchange_border(field):
    D = pltpu.SemaphoreType.DMA
    return pl.pallas_call(
        border_kernel,
        out_shape=jax.ShapeDtypeStruct((12, 10, 8, 128), jnp.bfloat16),
        in_specs=[VM], out_specs=VM,
        scratch_shapes=[D((8,)), D((8,))],
        compiler_params=pltpu.CompilerParams(collective_id=3, has_side_effects=True),
        name="exchange_border",
    )(field)


def reduce_kernel(
    g1_in, g2_in, misc_in, field_ref, g1_ref, g2_ref, misc_ref, wide_ref, part_ref,
    half_in, half, x_out, x_in, x_own, y_out, y_in, y_own, z_in, z_all,
    y_all, x_all, c_all, h_send, h_recv, c_send, c_recv, x_send, x_recv, y_send, y_recv, z_send, z_recv,
):
    core, x, y, z = place()
    partner = device(1 - core, x, y, z)
    xs = [device(core, (x + d) % 4, y, z) for d in range(1, 4)]
    ys = [device(core, x, (y + d) % 4, z) for d in range(1, 4)]
    zs = [device(core, x, y, (z + d) % 16) for d in range(1, 16)]
    barrier = pltpu.get_barrier_semaphore()
    for peer in [partner, *xs, *ys, *zs, *around()]:
        pl.semaphore_signal(barrier, inc=1, device_id=peer, device_id_type=MESH)
    pl.semaphore_wait(barrier, 30)
    part_ref[0:2304] = g1_in[...]
    part_ref[2304:3456] = g2_in[...]
    part_ref[3456:3480] = misc_in[...]
    part_ref[3480:ROWS] = jnp.zeros((ROWS - 3480, 128), jnp.float32)

    def copy(src, dst, send, recv, peer):
        one = pltpu.make_async_remote_copy(
            src_ref=src, dst_ref=dst, send_sem=send, recv_sem=recv,
            device_id=peer, device_id_type=MESH,
        )
        one.start()
        return one

    theirs = pl.multiple_of((1 - core) * HALF, HALF)
    mine = pl.multiple_of(core * HALF, HALF)
    c = copy(part_ref.at[pl.ds(theirs, HALF)], half_in, c_send.at[0], c_recv.at[0], partner)
    halo = exchange(field_ref, wide_ref, 6, 3, h_send, h_recv, 0)
    c.wait()
    total = part_ref[pl.ds(mine, HALF)] + half_in[...]
    half[...] = total
    x_out[...] = total.astype(jnp.bfloat16)
    cs = [
        copy(x_out.at[pl.ds(pl.multiple_of(((x + d) % 4) * QX, QX), QX)], x_in.at[d - 1],
             x_send.at[d - 1], x_recv.at[d - 1], xs[d - 1])
        for d in range(1, 4)
    ]
    total = half[pl.ds(pl.multiple_of(x * QX, QX), QX)]
    for d in range(3):
        cs[d].wait()
        total = total + x_in[d].astype(jnp.float32)
    x_own[...] = total
    y_out[...] = total.astype(jnp.bfloat16)
    cs = [
        copy(y_out.at[pl.ds(pl.multiple_of(((y + d) % 4) * QY, QY), QY)], y_in.at[d - 1],
             y_send.at[d - 1], y_recv.at[d - 1], ys[d - 1])
        for d in range(1, 4)
    ]
    total = x_own[pl.ds(pl.multiple_of(y * QY, QY), QY)]
    for d in range(3):
        cs[d].wait()
        total = total + y_in[d].astype(jnp.float32)
    y_own[...] = total
    cs = [
        copy(y_own.at[pl.ds(pl.multiple_of(((z + d) % 16) * QZ, QZ), QZ)], z_in.at[d - 1],
             z_send.at[d - 1], z_recv.at[d - 1], zs[d - 1])
        for d in range(1, 16)
    ]
    total = y_own[pl.ds(pl.multiple_of(z * QZ, QZ), QZ)]
    for d in range(15):
        cs[d].wait()
        total = total + z_in[d]
    own = pl.ds(pl.multiple_of(z * QZ, QZ), QZ)
    z_all[own] = total
    cs = [
        copy(z_all.at[own], z_all.at[own], z_send.at[14 + d], z_recv.at[14 + d], zs[d - 1])
        for d in range(1, 16)
    ]
    for one in cs:
        one.wait()
    own = pl.ds(pl.multiple_of(y * QY, QY), QY)
    y_all[own] = z_all[...].astype(jnp.bfloat16)
    cs = [
        copy(y_all.at[own], y_all.at[own], y_send.at[2 + d], y_recv.at[2 + d], ys[d - 1])
        for d in range(1, 4)
    ]
    for one in cs:
        one.wait()
    own = pl.ds(pl.multiple_of(x * QX, QX), QX)
    x_all[own] = y_all[...]
    cs = [
        copy(x_all.at[own], x_all.at[own], x_send.at[2 + d], x_recv.at[2 + d], xs[d - 1])
        for d in range(1, 4)
    ]
    for one in cs:
        one.wait()
    c = copy(x_all, c_all, c_send.at[1], c_recv.at[1], partner)
    for one in halo:
        one.wait()
    c.wait()
    first = core == 0
    low = jnp.where(first, x_all[...], c_all[...]).astype(jnp.float32)
    high = jnp.where(first, c_all[...], x_all[...]).astype(jnp.float32)
    g1_ref[0:HALF] = low
    g1_ref[HALF:2304] = high[0 : 2304 - HALF]
    g2_ref[...] = high[2304 - HALF : 3456 - HALF]
    misc_ref[...] = high[3456 - HALF : 3480 - HALF]


def all_reduce(g1, g2, misc, field):
    bf, f = jnp.bfloat16, jnp.float32
    V, D = pltpu.VMEM, pltpu.SemaphoreType.DMA
    shape = jax.ShapeDtypeStruct
    return pl.pallas_call(
        reduce_kernel,
        out_shape=(shape((2304, 128), f), shape((1152, 128), f), shape((24, 128), f), shape((20, 14, 8, 128), bf)),
        in_specs=[VM] * 4,
        out_specs=(VM,) * 4,
        scratch_shapes=[
            V((ROWS, 128), f),
            V((HALF, 128), f), V((HALF, 128), f), V((HALF, 128), bf), V((3, QX, 128), bf), V((QX, 128), f),
            V((QX, 128), bf), V((3, QY, 128), bf), V((QY, 128), f), V((15, QZ, 128), f), V((QY, 128), f),
            V((QX, 128), bf), V((HALF, 128), bf), V((HALF, 128), bf),
            D((8,)), D((8,)), D((2,)), D((2,)), D((6,)), D((6,)), D((6,)), D((6,)), D((30,)), D((30,)),
        ],
        compiler_params=pltpu.CompilerParams(collective_id=1, has_side_effects=True),
        name="all_reduce",
    )(g1, g2, misc, field)


def silu_grad(value, sig):
    return sig * (1.0 + value * (1.0 - sig))


def inside(shape, halo, width):
    row = lax.broadcasted_iota(jnp.int32, shape, 0) + (lax.axis_index("gx") * 8 - halo)
    lane = lax.broadcasted_iota(jnp.int32, shape, 1)
    col = lane // 4 + (lax.axis_index("gy") * 16 - halo)
    return (row >= 0) & (row < 256) & (col >= 0) & (col < 256) & (lane < width)


def dot(a, b, dims):
    return lax.dot_general(a, b, (dims, ((), ())), preferred_element_type=jnp.float32)


NN, NT, TN = ((1,), (0,)), ((1,), (1,)), ((0,), (0,))


def forward_kernel(
    st_ref, w1_ref, w2_ref, head_ref, near_ref,
    pre1_ref, patch1_ref, d2_ref, g2_ref, misc_ref, wide, hid, patch2,
):
    bf, f = jnp.bfloat16, jnp.float32
    wide[:, 0:80] = st_ref[...].astype(f)
    wide[:, 80:88] = jnp.zeros((12, 8, 256), f)
    for j in range(3):
        moved = wide[:, 4 * j : 4 * j + 80].astype(bf)
        for i in range(3):
            at = (3 * i + j) * 256
            patch1_ref[:, at : at + 256] = moved[i : i + 10].reshape(800, 256)
    pre1 = dot(patch1_ref[...], w1_ref[...], NN)
    pre1_ref[...] = pre1
    hidden = (pre1 * jax.nn.sigmoid(pre1)).astype(bf).astype(f).reshape(10, 80, 128)
    hid[...] = jnp.where(inside((10, 80, 128), 1, 72), hidden, 0.0)
    for j in range(3):
        moved = hid[:, 4 * j : 4 * j + 64].astype(bf)
        for i in range(3):
            at = (3 * i + j) * 128
            patch2[:, at : at + 128] = moved[i : i + 8].reshape(512, 128)
    pre2 = dot(patch2[...], w2_ref[...], NN)
    sig2 = jax.nn.sigmoid(pre2)
    hidden2 = (pre2 * sig2).astype(bf)
    z = dot(head_ref[...], hidden2, NT) - 2.19
    near = near_ref[...]
    real = lax.broadcasted_iota(jnp.int32, (16, 512), 0) < 10
    p = jax.nn.sigmoid(z)
    u = jnp.log1p(jnp.exp(-jnp.abs(z)))
    log_p = jnp.minimum(z, 0.0) - u
    log_q = jnp.minimum(-z, 0.0) - u
    q = 1.0 - p
    miss = 1.0 - jnp.where(near < FAR, jnp.exp(near * -0.125), 0.0)
    miss = miss * miss
    miss = miss * miss
    hit = near == 0.0
    loss = jnp.where(hit, -q * q * log_p, -miss * p * p * log_q)
    slope = jnp.where(hit, q * q * (2.0 * p * log_p - q), miss * p * p * (p - 2.0 * q * log_q))
    loss = jnp.where(real, loss, 0.0) * (1.0 / 256.0)
    slope = jnp.where(real, slope, 0.0) * (1.0 / 256.0)
    total = jnp.sum(jnp.sum(loss, axis=0, keepdims=True), axis=1, keepdims=True)
    d_z = slope.astype(bf)
    misc_ref[0:16] = dot(d_z, hidden2, NN)
    misc_ref[16:24] = jnp.broadcast_to(total, (8, 128))
    d_hid2 = dot(d_z, head_ref[...], TN)
    d2 = (d_hid2 * silu_grad(pre2, sig2)).astype(bf)
    d2_ref[...] = d2
    g2 = dot(d2, patch2[...], TN)
    for t in range(9):
        at = t * 128
        g2_ref[at : at + 128] = g2[:, at : at + 128].T


def forward(st, w1, w2, head, near):
    bf, f = jnp.bfloat16, jnp.float32
    shape, V = jax.ShapeDtypeStruct, pltpu.VMEM
    return pl.pallas_call(
        forward_kernel,
        out_shape=(
            shape((800, 128), f), shape((800, 2304), bf), shape((512, 128), bf), shape((1152, 128), f),
            shape((24, 128), f),
        ),
        in_specs=[VM] * 5, out_specs=(VM,) * 5,
        scratch_shapes=[V((12, 88, 256), f), V((10, 80, 128), f), V((512, 1152), bf)],
        name="forward",
    )(st, w1, w2, head, near)


def backward_kernel(
    d2_ref, pre1_ref, patch1_ref, w1_ref, w2_ref, g1_ref, cur_ref, al_ref, wide, wide1,
):
    bf, f = jnp.bfloat16, jnp.float32
    wide[:, 0:80] = jnp.where(inside((12, 80, 128), 2, 80), d2_ref[...].astype(f), 0.0)
    wide[:, 80:88] = jnp.zeros((12, 8, 128), f)
    d_hid1 = jnp.zeros((800, 128), f)
    for j in range(3):
        moved = wide[:, 8 - 4 * j : 88 - 4 * j].astype(bf)
        for i in range(3):
            at = (3 * i + j) * 128
            d_hid1 += dot(moved[2 - i : 12 - i].reshape(800, 128), w2_ref[at : at + 128], NT)
    pre1 = pre1_ref[...]
    d1 = d_hid1 * silu_grad(pre1, jax.nn.sigmoid(pre1))
    d1 = d1.astype(bf).astype(f).reshape(10, 80, 128)
    d1 = jnp.where(inside((10, 80, 128), 1, 72), d1, 0.0)
    wide1[...] = d1
    row = lax.broadcasted_iota(jnp.int32, (10, 80, 128), 0)
    lane = lax.broadcasted_iota(jnp.int32, (10, 80, 128), 1)
    tile = (row >= 1) & (row < 9) & (lane >= 4) & (lane < 68)
    own = jnp.where(tile, d1, 0.0).astype(bf).reshape(800, 128)
    g1 = dot(own, patch1_ref[...], TN)
    for t in range(18):
        at = t * 128
        g1_ref[at : at + 128] = g1[:, at : at + 128].T
    d_st = jnp.zeros((512, 256), f)
    for j in range(3):
        moved = wide1[:, 8 - 4 * j : 72 - 4 * j].astype(bf)
        for i in range(3):
            at = (3 * i + j) * 256
            d_st += dot(moved[2 - i : 10 - i].reshape(512, 128), w1_ref[at : at + 256], NT)
    cur_ref[...] = d_st[:, 0:128].astype(bf)
    al_ref[...] = d_st[:, 128:256].astype(bf)


def backward(d2, pre1, patch1, w1, w2):
    bf, f = jnp.bfloat16, jnp.float32
    shape, V = jax.ShapeDtypeStruct, pltpu.VMEM
    return pl.pallas_call(
        backward_kernel,
        out_shape=(shape((2304, 128), f), shape((512, 128), bf), shape((512, 128), bf)),
        in_specs=[VM] * 5, out_specs=(VM,) * 3,
        scratch_shapes=[V((12, 88, 128), f), V((10, 80, 128), f)],
        name="backward",
    )(d2, pre1, patch1, w1, w2)


def within(size, first, shift, limit):
    at = first + jnp.arange(size, dtype=jnp.int32)[:, None]
    return (at >= 0) & (at < limit) & (at + shift >= 0) & (at + shift < limit)


def slide(wide, rows, cols, starts):
    parts = [
        lax.dynamic_slice(wide[:, :, s], (starts[s, 0], starts[s, 1], jnp.int32(0)), (rows, cols, 128))
        for s in range(4)
    ]
    return jnp.stack(parts, axis=2)


def per_device(
    current, previous, offsets, center_rows, center_cols, classes, w_merge1, w_merge2, w_head
):
    bf = jnp.bfloat16
    row0, col0 = lax.axis_index("gx") * 8, lax.axis_index("gy") * 16
    n_cls = w_head.shape[1]
    cur = current.transpose(1, 2, 0, 3).reshape(8, 8, 8, 128)
    prev = previous.transpose(1, 2, 0, 3).reshape(8, 8, 8, 128)
    obj = jnp.concatenate([center_rows, center_cols, classes]).T.astype(jnp.float32)
    cur_wide, prev_wide, near = exchange_inputs(cur, prev, obj)
    zero = jnp.zeros((), bf)
    still = jnp.zeros((1, 4), jnp.int32)
    aligned = slide(prev_wide.reshape(24, 32, 4, 128), 12, 20, 6 - offsets)
    keep_rows = within(12, row0 - 2, -offsets[None, :, 0], 256)[:, None, :, None]
    keep_cols = within(20, col0 - 2, -offsets[None, :, 1], 256)[None, :, :, None]
    aligned = jnp.where(keep_rows & keep_cols, aligned, zero)
    on_rows = within(12, row0 - 2, still, 256)[:, None, :, None]
    on_cols = within(20, col0 - 2, still, 256)[None, :, :, None]
    near_cur = jnp.where(on_rows & on_cols, cur_wide.reshape(12, 20, 4, 128), zero)
    stacked = jnp.concatenate([near_cur, aligned], axis=3).reshape(12, 80, 256)
    w1, w2 = w_merge1.reshape(2304, 128), w_merge2.reshape(1152, 128)
    head = jnp.pad(w_head.T, ((0, 16 - n_cls), (0, 0)))
    pre1, patch1, d2, g2, misc = forward(stacked, w1, w2, head, near)
    d2 = exchange_border(d2.reshape(8, 8, 8, 128)).reshape(12, 80, 128)
    g1, g_cur, d_al = backward(d2, pre1, patch1, w1, w2)
    g1, g2, misc, back_wide = all_reduce(g1, g2, misc, d_al.reshape(8, 8, 8, 128))
    back = slide(back_wide.reshape(20, 28, 4, 128), 8, 16, 6 + offsets)
    keep_rows = within(8, row0, offsets[None, :, 0], 256)[:, None, :, None]
    keep_cols = within(16, col0, offsets[None, :, 1], 256)[None, :, :, None]
    grad_previous = jnp.where(keep_rows & keep_cols, back, zero).transpose(2, 0, 1, 3)
    grad_current = g_cur.reshape(8, 16, 4, 128).transpose(2, 0, 1, 3)
    return (
        misc[16, 0], g1.reshape(3, 3, 256, 128), g2.reshape(3, 3, 128, 128), misc[:n_cls].T,
        grad_current, grad_previous,
    )


def solution(mesh):
    placed = (
        P(None, "gx", "gy", None),
        P(None, "gx", "gy", None),
        P(),
        P(),
        P(),
        P(),
        P(),
        P(),
        P(),
    )
    return jax.shard_map(
        per_device,
        mesh=mesh,
        in_specs=placed,
        out_specs=(P(), P(), P(), P(), P(None, "gx", "gy", None), P(None, "gx", "gy", None)),
        check_vma=False,
    )
```

time: 270 us -> 183 us (0.68)
  the two profiles are of different devices: /device:TPU:7 before, /device:TPU:1 now
where the time goes in v2:
time: 183 us; the launch traced here: 182 us
  Pallas kernels  129 us (70%)
  between operations  31.1 us (17%)
  local copies, waits for them, and re-layouts  18 us (10%)
  other arithmetic  4.64 us (3%)
    pallas_call x1, Pallas kernels, all_reduce(): pl.pallas_call(reduce_kernel, out_shape=(shape((2304, 128), f), shape((11...  61.2 us
    pallas_call x1, Pallas kernels, exchange_inputs(): pl.pallas_call(inputs_kernel, out_shape=(shape((12, 10, 8, 128), jnp.bflo...  39 us
    pallas_call x1, Pallas kernels, exchange_border(): pl.pallas_call(border_kernel, out_shape=jax.ShapeDtypeStruct((12, 10, 8,...  16.4 us
    slice x2, local copies, waits for them, and re-layouts, slide(): wide[:, :, s]  6.63 us
    pallas_call x1, Pallas kernels, backward(): pl.pallas_call(backward_kernel, out_shape=(shape((2304, 128), f), shape((...  6.41 us
    pallas_call x1, Pallas kernels, forward(): pl.pallas_call(forward_kernel, out_shape=(shape((800, 128), f), shape((80...  5.5 us

profile of v2, /device:TPU:1, one launch (start us, length us, event | category | flops | bytes accessed | tf_op | source)
XLA Modules:
  0.0 182.3 jit_solution(9260084559543053883)
XLA Ops:
  0.6 0.7 broadcast_add_fusion
  1.3 0.7 fusion.14
  9.7 1.7 copy.45
  11.4 1.7 copy.46
  13.1 0.7 add_convert_fusion
  13.8 0.7 copy.47
  14.5 39.0 %exchange_inputs.1 = (bf16[12,10,8,128]{3,2,1,0:T(8,128)(2,1)}, bf16[24,16,8,128]{3,2,1,0:T(8,128)(2,1)}, f32[16,512]{1,0:T(8,128)}) custom-call(bf16[8,8,8,128]{3,2,1,0:T(8,128)(2,1)} %bitcast.62, bf16[8,8,8,128]{3,2,1,0:T(8,128)(2,1)} %bitcast.63, f32[64,12]{1,0:T(8,128)} %bitcast.65), custom_call_target="tpu_custom_call" | custom-call | tf_op jit(solution)/shard_map/exchange_inputs/pallas_call | solution.py:79
  53.5 3.7 %fusion.11 = (bf16[24,32,1,128]{3,2,1,0:T(2,128)(2,1)S(1)}, bf16[24,32,1,128]{3,2,1,0:T(2,128)(2,1)S(1)}, bf16[24,32,1,128]{3,2,1,0:T(2,128)(2,1)S(1)}, bf16[24,32,1,128]{3,2,1,0:T(2,128)(2,1)S(1)}) fusion(bf16[24,32,4,128]{3,2,1,0:T(4,128)(2,1)} %bitcast.52), kind=kLoop, calls=%fused_computation.52 | loop fusion | bytes 1572864 | tf_op jit(solution)/shard_map/slice | solution.py:373
  57.3 0.0 copy-start.4
  57.3 0.0 copy-start.2
  57.3 0.3 constant_dynamic-slice_fusion.6
  65.0 0.3 constant_dynamic-slice_fusion.4
  65.2 0.6 pad_maximum_fusion.1
  65.8 0.0 copy-start.6
  65.9 0.1 fusion.2
  66.0 0.1 fusion.4
  66.1 0.1 copy.48
  66.2 0.1 and.223
  66.3 0.1 broadcast_and_fusion
  66.4 0.1 copy.49
  66.5 0.2 broadcast_select_fusion
  66.7 0.1 and.211
  66.8 0.1 and.212
  66.9 0.1 broadcast_and_fusion.2
  67.0 0.2 bitcast_select_fusion
  67.2 0.8 pad_maximum_fusion.st_ref
  68.0 0.6 pad.4.head_ref
  68.6 5.5 %forward.1 = (f32[800,128]{1,0:T(8,128)}, bf16[800,2304]{1,0:T(8,128)(2,1)}, bf16[512,128]{1,0:T(8,128)(2,1)}, f32[1152,128]{1,0:T(8,128)}, f32[24,128]{1,0:T(8,128)}) custom-call(bf16[12,80,256]{2,1,0:T(8,128)(2,1)} %pad_maximum_fusion.st_ref, bf16[2304,128]{1,0:T(8,128)(2,1)} %bitcast.53, bf16[1152,128]{1,0:T(8,128)(2,1)} %bitcast.56, ...), custom_call_target="tpu_custom_call" | custom-call | tf_op jit(solution)/shard_map/forward/pallas_call | solution.py:307
  74.1 16.4 %exchange_border.1 = bf16[12,10,8,128]{3,2,1,0:T(8,128)(2,1)} custom-call(bf16[8,8,8,128]{3,2,1,0:T(8,128)(2,1)} %bitcast.64), custom_call_target="tpu_custom_call" | custom-call | tf_op jit(solution)/shard_map/exchange_border/pallas_call | solution.py:100
  90.5 6.4 %backward.1 = (f32[2304,128]{1,0:T(8,128)}, bf16[512,128]{1,0:T(8,128)(2,1)}, bf16[512,128]{1,0:T(8,128)(2,1)}) custom-call(bf16[12,80,128]{2,1,0:T(8,128)(2,1)} %bitcast.60, f32[800,128]{1,0:T(8,128)} %get-tuple-element.25.pre1_ref, bf16[800,2304]{1,0:T(8,128)(2,1)} %get-tuple-element.26.patch1_ref, bf16[2304,128]{1,0:T(8,128)(2,1)} %bitcast.54, ...), custom_call_target="tpu_custom_call" | custom-call | tf_op jit(solution)/shard_map/backward/pallas_call | solution.py:357
  96.9 61.2 %all_reduce.1 = (f32[2304,128]{1,0:T(8,128)}, f32[1152,128]{1,0:T(8,128)}, f32[24,128]{1,0:T(8,128)}, bf16[20,14,8,128]{3,2,1,0:T(8,128)(2,1)}) custom-call(f32[2304,128]{1,0:T(8,128)} %get-tuple-element.27.g1_in, f32[1152,128]{1,0:T(8,128)} %get-tuple-element.28.g2_in, f32[24,128]{1,0:T(8,128)} %get-tuple-element.29.misc_in, bf16[8,8,8,128]{3,2,1,0:T(8,128)(2,1)} %bitcast.70), custom_call_target="tpu_custom_call" | custom-call | tf_op jit(solution)/shard_map/all_reduce/pallas_call | solution.py:216
  158.2 2.9 %fusion.12 = (bf16[20,28,1,128]{3,2,1,0:T(2,128)(2,1)S(1)}, bf16[20,28,1,128]{3,2,1,0:T(2,128)(2,1)S(1)}, bf16[20,28,1,128]{3,2,1,0:T(2,128)(2,1)S(1)}, bf16[20,28,1,128]{3,2,1,0:T(2,128)(2,1)S(1)}) fusion(bf16[20,28,4,128]{3,2,1,0:T(4,128)(2,1)} %bitcast.55), kind=kLoop, calls=%fused_computation.53 | loop fusion | bytes 1146880 | tf_op jit(solution)/shard_map/slice | solution.py:373
  161.0 0.0 copy-start.3
  161.1 0.6 fusion.13
  165.5 0.1 constant_dynamic-slice_fusion.3
  169.1 0.1 constant_dynamic-slice_fusion.2
  173.0 0.1 constant_dynamic-slice_fusion.1
  177.0 0.1 constant_dynamic-slice_fusion
  177.2 0.1 fusion.6
  177.2 0.1 fusion.8
  177.3 0.1 broadcast_and_fusion.1
  177.4 0.8 fusion
  178.2 0.6 slice_bitcast_fusion
  178.8 0.5 slice.100
  179.3 0.7 copy.64
  180.0 1.0 copy.67
  181.0 0.5 copy-done.1
  181.5 0.8 copy.68
  (24 shorter events, 0.1 us)
Async XLA Ops:
  57.3 8.6 %copy-start.4 = (s32[4,2]{0,1:T(2,128)S(1)}, s32[4,2]{0,1:T(2,128)}, u32[]{:S(2)}) copy-start(s32[4,2]{0,1:T(2,128)} %param.11) | copy-start | bytes 100
  57.3 9.7 %copy-start.2 = (bf16[12,10,8,128]{3,2,1,0:T(8,128)(2,1)S(1)}, bf16[12,10,8,128]{3,2,1,0:T(8,128)(2,1)}, u32[]{:S(2)}) copy-start(bf16[12,10,8,128]{3,2,1,0:T(8,128)(2,1)} %get-tuple-element.21) | copy-start | bytes 737284
  65.8 2.2 %copy-start.6 = (bf16[128,10]{0,1:T(8,128)(2,1)S(1)}, bf16[128,10]{0,1:T(8,128)(2,1)}, u32[]{:S(2)}) copy-start(bf16[128,10]{0,1:T(8,128)(2,1)} %param.17) | copy-start | bytes 7684
  158.1 20.1 %copy-start.5 = (f32[24,128]{1,0:T(8,128)S(1)}, f32[24,128]{1,0:T(8,128)}, u32[]{:S(2)}) copy-start(f32[24,128]{1,0:T(8,128)} %get-tuple-element.31) | copy-start | bytes 36868
  161.0 18.3 %copy-start.3 = (bf16[512,128]{1,0:T(8,128)(2,1)S(1)}, bf16[512,128]{1,0:T(8,128)(2,1)}, u32[]{:S(2)}) copy-start(bf16[512,128]{1,0:T(8,128)(2,1)} %get-tuple-element.34) | copy-start | bytes 393220
  161.1 18.9 %copy-start = (f32[2304,128]{1,0:T(8,128)S(1)}, f32[2304,128]{1,0:T(8,128)}, u32[]{:S(2)}) copy-start(f32[2304,128]{1,0:T(8,128)} %get-tuple-element.32) | copy-start | bytes 3538948
  180.0 1.5 copy-start.1
